TPU v7x, 32 devices: a whole 2x2x4 slice. The times are simulated.
32 devices in a mesh: ens: 2 (over y), wave: 4 (over z), lev: 2 (over x), pot: 2 (over core).
Axes of the slice: x: 2, y: 2, z: 4, core: 2. Of those that a mesh axis runs over, the one named last changes fastest.
Arguments:
- spectra: bfloat16 [4, 64, 2, 64, 512], P(('ens', 'pot'), 'wave', None, 'lev'), parts along dimension 0, may hold values from -0.1875 to 0.1875
- legendre: bfloat16 [64, 768, 512], P('wave', 'lev'), may hold values from -0.25 to 0.25
- row_map: int32 [4, 32], replicated, may hold values from 0 to 767, as said below
- seg_map: int32 [4, 32], replicated, may hold values from 0 to 11
- interp: bfloat16 [4, 32, 128, 128], P('wave'), may hold values from -0.5 to 0.5
- edges: int32 [4, 4, 12288], P('wave'), may hold values from 0 to 4351, as said below
- inv_len: float32 [4, 2, 12288], P('wave'), may hold values from 0.5 to 2
Outputs:
- normal_wind: bfloat16 [128, 49152], P(('ens', 'lev', 'pot'), 'wave'), parts along dimension 0
There are 2 independent parts, one for each index of `ens`. A program takes and returns all parts, laid end to end along the dimension named above; an argument that names none is the same for every part. Nothing has to cross between parts.
Inputs may be any that keep to these rules, and one draw needn't show every extreme that they name: For each patch q and each band b of rows b * 192 to b * 192 + 191, at most 24 entries of row_map[q, :] lie in band b, and every patch has exactly 24 entries in some band. edges[q, 0, e] lies in 128 to 4223, and edges[q, 1, e], edges[q, 2, e], edges[q, 3, e] each lie within 128 of it.
All inputs are finite; a program needn't handle non-finite values.
Results may differ from a plain program's by a relative error of at most 0.0068.
Values may be sent and summed in bfloat16 or wider, within the bound.
No kernel may reach another device: no remote copies, remote signals or barrier semaphores. Data moves between devices by JAX's collectives and lax.ppermute only.
A program may use at most 128 MiB of HBM per device.

v0:
```python
import math

import jax
import jax.numpy as jnp
from jax import lax
from jax.sharding import PartitionSpec as P

NLON = 1536
BLOCK = 128
HALO = 128


def extended_2(cells, sides, width):
    for axis, dim in sides:
        count = lax.axis_size(axis)
        head = lax.slice_in_dim(cells, 0, width, axis=dim)
        tail = lax.slice_in_dim(cells, cells.shape[dim] - width, cells.shape[dim], axis=dim)
        cells = jnp.concatenate(
            [
                lax.ppermute(tail, axis, [(i, (i + 1) % count) for i in range(count)]),
                cells,
                lax.ppermute(head, axis, [((i + 1) % count, i) for i in range(count)]),
            ],
            axis=dim,
        )
    return cells


def fourier_matrix(wave_count, longitude_count):
    wave_index = lax.broadcasted_iota(jnp.int32, (wave_count, longitude_count), 0)
    lon_index = lax.broadcasted_iota(jnp.int32, (wave_count, longitude_count), 1)
    angle_values = (wave_index * lon_index % longitude_count).astype(jnp.float32) * (
        2.0 * math.pi / longitude_count
    )
    factor = jnp.where(wave_index == 0, 1.0, 2.0).astype(jnp.float32)
    return jnp.stack(
        [factor * jnp.cos(angle_values), -factor * jnp.sin(angle_values)], axis=0
    ).astype(jnp.bfloat16)


def body(spectra, legendre, row_map, seg_map, interp, edges, inv_len):
    own_spectra = spectra[0]
    spectral = jnp.einsum(
        "mrj,mclj->lrcm",
        legendre,
        lax.all_gather(own_spectra, "lev", axis=2, tiled=True),
        preferred_element_type=jnp.float32,
    ).astype(jnp.bfloat16)
    banded = lax.all_to_all(
        lax.all_to_all(spectral, "lev", split_axis=0, concat_axis=1, tiled=True),
        "wave",
        split_axis=1,
        concat_axis=3,
        tiled=True,
    )
    fourier_modes = fourier_matrix(banded.shape[3], NLON)
    grid_field = jnp.einsum(
        "lrcm,cmk->lrk", banded, fourier_modes, preferred_element_type=jnp.float32
    ).astype(jnp.bfloat16)
    level_count = grid_field.shape[0]
    rows_dev = grid_field.shape[1]
    segments = NLON // BLOCK
    blocks_dev = row_map.shape[1]
    patch_count = lax.axis_size("wave")
    capacity = min(blocks_dev, max(3, 3 * blocks_dev // patch_count))
    own_band = lax.axis_index("wave")
    row_band = row_map // rows_dev
    is_mine = (row_band == own_band).astype(jnp.int32)
    slot_rank = jnp.cumsum(is_mine, axis=1) - is_mine
    slot_ids = jnp.arange(capacity, dtype=jnp.int32)
    slot_hit = (is_mine[:, :, None] == 1) & (slot_rank[:, :, None] == slot_ids[None, None, :])
    piece_index = row_map % rows_dev * segments + seg_map
    source_index = jnp.sum(jnp.where(slot_hit, piece_index[:, :, None], 0), axis=1)
    pieces = grid_field.reshape(level_count, rows_dev * segments, BLOCK)
    outgoing = jnp.take(pieces, source_index.reshape(-1), axis=1)
    incoming = lax.all_to_all(outgoing, "wave", split_axis=1, concat_axis=1, tiled=True)
    own_rows = lax.dynamic_index_in_dim(row_map, own_band, 0, keepdims=False)
    own_row_band = own_rows // rows_dev
    block_ids = jnp.arange(blocks_dev, dtype=jnp.int32)
    same_band = own_row_band[:, None] == own_row_band[None, :]
    earlier = block_ids[None, :] < block_ids[:, None]
    own_rank = jnp.sum((same_band & earlier).astype(jnp.int32), axis=1)
    arrival = own_row_band * capacity + own_rank
    gathered = jnp.take(incoming, arrival, axis=1)
    cell_field = jnp.einsum(
        "kij,lkj->lki", interp[0], gathered, preferred_element_type=jnp.float32
    ).astype(jnp.bfloat16)
    cell_field = cell_field.reshape(level_count, blocks_dev * BLOCK)
    extended = extended_2(cell_field, (("wave", 1),), HALO)
    edge_ids = edges[0]
    lengths = inv_len[0]
    pot_index = lax.axis_index("pot")
    first_cell = jnp.where(pot_index == 0, edge_ids[2], edge_ids[0])
    second_cell = jnp.where(pot_index == 0, edge_ids[3], edge_ids[1])
    weights_edge = jnp.where(pot_index == 0, -lengths[1], lengths[0])
    edge_term = (
        jnp.take(extended, second_cell, axis=1).astype(jnp.float32)
        - jnp.take(extended, first_cell, axis=1).astype(jnp.float32)
    ) * weights_edge
    normal_wind = lax.psum_scatter(edge_term, "pot", scatter_dimension=0, tiled=True).astype(
        jnp.bfloat16
    )
    return normal_wind


def solution(mesh):
    return jax.shard_map(
        body,
        mesh=mesh,
        in_specs=(
            P(("ens", "pot"), "wave", None, "lev", None),
            P("wave", "lev", None),
            P(),
            P(),
            P("wave", None, None, None),
            P("wave", None, None),
            P("wave", None, None),
        ),
        out_specs=P(("ens", "lev", "pot"), "wave"),
        check_vma=False,
    )
```

profile of v0, /device:TPU:0, one launch (start us, length us, event | category | flops | bytes accessed | tf_op | source)
XLA Modules:
  0.0 373.4 jit_solution(1620999810213235277)
XLA Ops:
  10.2 2.2 broadcast_select_fusion.2
  12.3 32.4 %all-gather.3.cloned.1.call-done = bf16[1,16,2,64,512]{4,3,2,1,0:T(8,128)(2,1)} async-done(((bf16[1,16,2,32,512]{4,3,2,1,0:T(8,128)(2,1)}), bf16[1,16,2,64,512]{4,3,2,1,0:T(8,128)(2,1)}) %all-gather.3.cloned.1.call-update) | async-done | bytes 2097168 | tf_op jit(solution)/shard_map/all_gather | solution.py:46
  44.7 5.4 %fusion.8 = bf16[64,384,2,16]{1,0,2,3:T(8,128)(2,1)S(1)} fusion(bf16[16,384,512]{2,1,0:T(8,128)(2,1)} %param.10, bf16[1,16,2,64,512]{4,3,2,1,0:T(8,128)(2,1)} %all-gather.3.cloned.1.call-done), kind=kOutput, calls=%fused_computation.10 | convolution fusion | flops 806092800 | bytes 9961472 | tf_op jit(solution)/shard_map/mrj,mclj->lrcm/dot_general | solution.py:43
  50.1 2.8 copy.47
  52.9 3.7 all-to-all-start
  58.3 17.6 %all-to-all-done = bf16[64,384,2,16]{1,2,3,0:T(2,128)(2,1)S(1)} async-done(((bf16[64,384,2,16]{1,2,3,0:T(2,128)(2,1)}), bf16[64,384,2,16]{1,2,3,0:T(2,128)(2,1)S(1)}, u32[]{:S(2)}, u32[]{:S(2)}) %all-to-all-start) | async-done | bytes 1572896 | tf_op jit(solution)/shard_map/all_to_all | solution.py:50
  75.9 8.6 %copy.59 = bf16[32,2,384,2,16]{0,4,3,2,1:T(8,128)(2,1)} copy(bf16[32,2,384,2,16]{2,3,4,0,1:T(2,128)(2,1)S(1)} %bitcast.87) | data formatting | bytes 3145728 | tf_op jit(solution)/shard_map/all_to_all | solution.py:50
  84.5 8.3 %reshape.312 = bf16[4,2,98304]{2,1,0:T(2,128)(2,1)} reshape(bf16[768,2,16,32]{3,2,1,0:T(8,128)(2,1)} %bitcast.83) | data formatting | bytes 3145728
  92.8 4.7 %all-to-all-start.1 = ((bf16[4,2,98304]{2,1,0:T(2,128)(2,1)}), bf16[4,2,98304]{2,1,0:T(2,128)(2,1)S(1)}, u32[]{:S(2)}, u32[]{:S(2)}) async-start(bf16[4,2,98304]{2,1,0:T(2,128)(2,1)} %reshape.312), calls=%async_computation.1 | async-start | bytes 3145728 | tf_op jit(solution)/shard_map/all_to_all | solution.py:49
  98.2 35.2 %all-to-all-done.1 = bf16[4,2,98304]{2,1,0:T(2,128)(2,1)S(1)} async-done(((bf16[4,2,98304]{2,1,0:T(2,128)(2,1)}), bf16[4,2,98304]{2,1,0:T(2,128)(2,1)S(1)}, u32[]{:S(2)}, u32[]{:S(2)}) %all-to-all-start.1) | async-done | bytes 1572896 | tf_op jit(solution)/shard_map/all_to_all | solution.py:49
  133.5 4.6 %reshape.313 = bf16[768,2,16,32]{3,2,1,0:T(8,128)(2,1)} reshape(bf16[4,2,98304]{2,1,0:T(2,128)(2,1)S(1)} %all-to-all-done.1) | data formatting | bytes 3145728
  138.1 10.1 %copy.60 = bf16[32,4,192,2,16]{2,1,4,3,0:T(4,128)(2,1)S(1)} copy(bf16[32,4,192,2,16]{0,4,3,2,1:T(8,128)(2,1)} %bitcast.84) | data formatting | bytes 3145728 | tf_op jit(solution)/shard_map/all_to_all | solution.py:49
  148.7 9.1 %bitcast_convert_fusion = bf16[32,192,1536]{2,1,0:T(8,128)(2,1)} fusion(bf16[32,192,2,64]{1,3,2,0:T(8,128)(2,1)S(1)} %bitcast.85, bf16[1,64,1536]{2,1,0:T(8,128)(2,1)S(1)} %get-tuple-element.15, bf16[1,64,1536]{2,1,0:T(8,128)(2,1)S(1)} %get-tuple-element.16), kind=kOutput, calls=%fused_computation.4 | convolution fusion | flops 2425552896 | bytes 20840448 | tf_op jit(solution)/shard_map/lrcm,cmk->lrk/dot_general | solution.py:57
  157.8 35.2 %reshape.265 = bf16[32,2304,128]{2,1,0:T(8,128)(2,1)} reshape(bf16[32,192,1536]{2,1,0:T(8,128)(2,1)} %bitcast_convert_fusion) | data formatting | bytes 37748736 | tf_op jit(solution)/shard_map/reshape | solution.py:74
  193.0 20.7 %copy.52 = bf16[32,2304,128]{2,0,1:T(8,128)(2,1)} copy(bf16[32,2304,128]{2,1,0:T(8,128)(2,1)} %reshape.265) | data formatting | bytes 37748736 | tf_op jit(solution)/shard_map/reshape | solution.py:74
  213.7 7.1 %gather_fusion = bf16[96,32,128]{2,1,0:T(8,128)(2,1)S(1)} fusion(bf16[32,2304,128]{2,0,1:T(8,128)(2,1)} %copy.52, s32[1024]{0:T(1024)S(1)} %pad_clamp_fusion.1), kind=kCustom, calls=%fused_computation.2 | custom fusion | bytes 1573248 | tf_op jit(solution)/shard_map/jit(_take)/gather | solution.py:75
  221.9 3.5 all-to-all-start.2
  225.6 19.5 %all-to-all-done.2 = bf16[32,96,128]{2,0,1:T(8,128)(2,1)S(1)} async-done(((bf16[32,96,128]{2,0,1:T(8,128)(2,1)}), bf16[32,96,128]{2,0,1:T(8,128)(2,1)S(1)}, u32[]{:S(2)}, u32[]{:S(2)}) %all-to-all-start.2) | async-done | bytes 786464 | tf_op jit(solution)/shard_map/all_to_all | solution.py:76
  250.1 3.3 collective-permute-done
  253.9 43.3 %gather_fusion.3 = bf16[12288,32]{1,0:T(8,128)(2,1)} fusion(bf16[32,4352]{0,1:T(8,128)(2,1)S(1)} %copy.54, s32[12288]{0:T(1024)S(1)} %fusion.28), kind=kCustom, calls=%fused_computation.1.clone | custom fusion | bytes 1622016 | tf_op jit(solution)/shard_map/jit(_take)/gather | solution.py:98
  297.3 43.3 %gather_fusion.2 = bf16[12288,32]{1,0:T(8,128)(2,1)} fusion(bf16[32,4352]{0,1:T(8,128)(2,1)S(1)} %copy.54, s32[12288]{0:T(1024)S(1)} %fusion.27), kind=kCustom, calls=%fused_computation.clone | custom fusion | bytes 1622016 | tf_op jit(solution)/shard_map/jit(_take)/gather | solution.py:97
  340.5 12.1 %subtract_multiply_fusion = f32[32,12288]{0,1:T(8,128)} fusion(bf16[12288,32]{1,0:T(8,128)(2,1)} %gather_fusion.3, bf16[12288,32]{1,0:T(8,128)(2,1)} %gather_fusion.2, f32[12288]{0:T(1024)S(1)} %bitcast.94, pred[12288]{0:T(1024)(128)(4,1)S(1)} %get-tuple-element.17, pred[12288]{0:T(1024)(128)(4,1)S(1)} %get-tuple-element.18), kind=kLoop, calls=%fused_computation.7 | loop fusion | flops 2359296 | bytes 3219456 | tf_op jit(solution)/shard_map/mul | solution.py:96
  352.6 5.5 %copy.61 = f32[32,12288]{1,0:T(8,128)} copy(f32[32,12288]{0,1:T(8,128)} %subtract_multiply_fusion) | data formatting | bytes 3145728
  358.2 6.4 %reduce-scatter.4.cloned.1.call-done = f32[16,12288]{1,0:T(8,128)} async-done(((f32[32,12288]{1,0:T(8,128)}), f32[16,12288]{1,0:T(8,128)}) %reduce-scatter.4.cloned.1.call-update) | async-done | bytes 786448 | tf_op jit(solution)/shard_map/reduce_scatter | solution.py:100
  (53 shorter events, 15.2 us)
Async XLA Ops:
  6.5 239.1 %copy-start = (bf16[1,32,128,128]{3,2,1,0:T(8,128)(2,1)S(1)}, bf16[1,32,128,128]{3,2,1,0:T(8,128)(2,1)}, u32[]{:S(2)}) copy-start(bf16[1,32,128,128]{3,2,1,0:T(8,128)(2,1)} %param.13) | copy-start | bytes 3145732
  6.5 38.2 %all-gather.3.cloned.1.call-start = ((), (), s32[]{:S(2)}) async-start(), calls=%async_computation.4 | async-start | bytes 3145728 | tf_op jit(solution)/shard_map/all_gather | solution.py:46
  10.2 46.4 %copy-start.5 = (s32[32]{0:T(128)}, s32[32]{0:T(128)S(1)}, u32[]{:S(2)}) copy-start(s32[32]{0:T(128)S(1)} %convert_reduce_fusion) | copy-start | bytes 388
  52.9 23.0 %all-to-all-start = ((bf16[64,384,2,16]{1,2,3,0:T(2,128)(2,1)}), bf16[64,384,2,16]{1,2,3,0:T(2,128)(2,1)S(1)}, u32[]{:S(2)}, u32[]{:S(2)}) async-start(bf16[64,384,2,16]{1,2,3,0:T(2,128)(2,1)} %copy.47), calls=%async_computation | async-start | bytes 3145728 | tf_op jit(solution)/shard_map/all_to_all | solution.py:50
  92.8 4.7 %copy-start.4 = (f32[1,2,12288]{2,1,0:T(2,128)S(1)}, f32[1,2,12288]{2,1,0:T(2,128)}, u32[]{:S(2)}) copy-start(f32[1,2,12288]{2,1,0:T(2,128)} %param.15) | copy-start | bytes 294916
  92.8 40.7 %all-to-all-start.1 = ((bf16[4,2,98304]{2,1,0:T(2,128)(2,1)}), bf16[4,2,98304]{2,1,0:T(2,128)(2,1)S(1)}, u32[]{:S(2)}, u32[]{:S(2)}) async-start(bf16[4,2,98304]{2,1,0:T(2,128)(2,1)} %reshape.312), calls=%async_computation.1 | async-start | bytes 3145728 | tf_op jit(solution)/shard_map/all_to_all | solution.py:49
  213.7 11.7 %copy-start.6 = (s32[32]{0:T(128)S(1)}, s32[32]{0:T(128)}, u32[]{:S(2)}) copy-start(s32[32]{0:T(128)} %copy-done.5) | copy-start | bytes 388
  213.7 11.8 %copy-start.2 = (s32[1,1,12288]{2,1,0:T(1,128)S(1)}, s32[1,1,12288]{2,1,0:T(1,128)}, u32[]{:S(2)}) copy-start(s32[1,1,12288]{2,1,0:T(1,128)} %get-tuple-element.14) | copy-start | bytes 147460
  213.7 11.8 %copy-start.1 = (s32[1,1,12288]{2,1,0:T(1,128)S(1)}, s32[1,1,12288]{2,1,0:T(1,128)}, u32[]{:S(2)}) copy-start(s32[1,1,12288]{2,1,0:T(1,128)} %get-tuple-element.13) | copy-start | bytes 147460
  221.9 23.1 %all-to-all-start.2 = ((bf16[32,96,128]{2,0,1:T(8,128)(2,1)}), bf16[32,96,128]{2,0,1:T(8,128)(2,1)S(1)}, u32[]{:S(2)}, u32[]{:S(2)}) async-start(bf16[32,96,128]{2,0,1:T(8,128)(2,1)} %select_bitcast_fusion), calls=%async_computation.2 | async-start | bytes 1572864 | tf_op jit(solution)/shard_map/all_to_all | solution.py:76
  225.4 139.2 %reduce-scatter.4.cloned.1.call-start = ((), (), s32[]{:S(2)}) async-start(), calls=%async_computation.5 | async-start | bytes 2359296 | tf_op jit(solution)/shard_map/reduce_scatter | solution.py:100
  246.4 3.7 collective-permute-start.1
  247.9 5.4 %collective-permute-start = (bf16[32,128]{1,0:T(8,128)(2,1)S(1)}, bf16[32,128]{1,0:T(8,128)(2,1)S(1)}, u32[]{:S(2)}, u32[]{:S(2)}) collective-permute-start(bf16[32,128]{1,0:T(8,128)(2,1)S(1)} %get-tuple-element.11), channel_id=1, source_target_pairs={{0,4},{4,8},{8,12},{12,0},{1,5},{5,9},{9,13},{13,1},{2,6},{6,10},{... | collective-permute-start | bytes 24584 | tf_op jit(solution)/shard_map/ppermute | solution.py:20
  297.3 43.3 %copy-start.3 = (f32[1,1,12288]{2,1,0:T(1,128)S(1)}, f32[1,1,12288]{2,1,0:T(1,128)}, u32[]{:S(2)}) copy-start(f32[1,1,12288]{2,1,0:T(1,128)} %broadcast_select_fusion) | copy-start | bytes 147460
Sparse Core Ops, SparseCore 0:
  8.9 35.8 all-gather.2
  358.3 6.2 reduce-scatter.3
where the time goes:
time: 375 us; the launch traced here: 373 us
  local copies, waits for them, and re-layouts  191 us (51%)
  waiting for transfers between devices  117 us (31%)
  other arithmetic  22.4 us (6%)
  matrix products  15.2 us (4%)
  starting transfers between devices  14 us (4%)
  between operations  13.6 us (4%)
    reshape x2, local copies, waits for them, and re-layouts, body(): pieces = grid_field.reshape(level_count, rows_dev * segments, BLOCK)  55.9 us
    gather x1, local copies, waits for them, and re-layouts, body(): jnp.take(extended, first_cell, axis=1).astype(jnp.float32)  43.3 us
    gather x1, local copies, waits for them, and re-layouts, body(): jnp.take(extended, second_cell, axis=1).astype(jnp.float32)  43.3 us
    all_to_all x1, waiting for transfers between devices, body(): lax.all_to_all(lax.all_to_all(spectral, 'lev', split_axis=0, concat_axis=...  35.2 us
    all_gather x1, waiting for transfers between devices, body(): lax.all_gather(own_spectra, 'lev', axis=2, tiled=True)  32.4 us
    all_to_all x1, waiting for transfers between devices, body(): lax.all_to_all(outgoing, 'wave', split_axis=1, concat_axis=1, tiled=True)  19.5 us
    unnamed x17, local copies, waits for them, and re-layouts  18.5 us
    all_to_all x1, waiting for transfers between devices, body(): lax.all_to_all(spectral, 'lev', split_axis=0, concat_axis=1, tiled=True)  17.6 us
  transfers between devices with their start and end apart: 7, of which 7 were waited for; matrix products, arithmetic and copies ran while one was open for 2% of the time, Pallas kernels for 0%

commit v1 on v0

v1 whole, which is shorter than its diff:
```python
import functools
import math

import jax
import jax.numpy as jnp
from jax import lax
from jax.experimental import pallas as pl
from jax.experimental.pallas import tpu as pltpu
from jax.sharding import PartitionSpec as P

NLON = 1536
BLOCK = 128
HALO = 128
SUB = 8
LANE = 128
WHOLE = pl.BlockSpec(memory_space=pltpu.VMEM)
SCALARS = pl.BlockSpec(memory_space=pltpu.SMEM)


def dot_nt(a, b):
    return lax.dot_general(a, b, (((1,), (1,)), ((), ())), preferred_element_type=jnp.float32)


def select_kernel(where_ref, rows_ref, legendre_ref, out_ref, onehot_ref):
    patches, blocks = rows_ref.shape
    rows_dev = legendre_ref.shape[1]

    @pl.when(pl.program_id(0) == 0)
    def _():
        first = where_ref[1]
        eye = lax.broadcasted_iota(jnp.int32, (blocks, blocks), 0) == lax.broadcasted_iota(
            jnp.int32, (blocks, blocks), 1
        )
        columns = []
        for q in range(patches):
            row = (rows_ref[q : q + 1, :] - first).astype(jnp.float32)
            columns.append(jnp.sum(jnp.where(eye, row, 0.0), axis=1, keepdims=True))
        lane = lax.broadcasted_iota(jnp.int32, (SUB, rows_dev), 1).astype(jnp.float32)
        step = 0
        for g in range(blocks // SUB):
            for q in range(patches):
                part = columns[q][g * SUB : (g + 1) * SUB]
                onehot_ref[step * SUB : (step + 1) * SUB, :] = jnp.where(
                    part == lane, 1.0, 0.0
                ).astype(jnp.bfloat16)
                step += 1

    out_ref[0] = jnp.dot(
        onehot_ref[...], legendre_ref[0], preferred_element_type=jnp.float32
    ).astype(jnp.bfloat16)


def select_rows(legendre, row_map, first_wave, first_row, wave_count):
    _, rows_dev, degrees = legendre.shape
    patches, blocks = row_map.shape
    entries = patches * blocks
    return pl.pallas_call(
        select_kernel,
        out_shape=jax.ShapeDtypeStruct((wave_count, entries, degrees), jnp.bfloat16),
        grid_spec=pltpu.PrefetchScalarGridSpec(
            num_scalar_prefetch=1,
            grid=(wave_count,),
            in_specs=[
                pl.BlockSpec((patches, blocks), lambda i, where: (0, 0)),
                pl.BlockSpec((1, rows_dev, degrees), lambda i, where: (where[0] + i, 0, 0)),
            ],
            out_specs=pl.BlockSpec((1, entries, degrees), lambda i, where: (i, 0, 0)),
            scratch_shapes=[pltpu.VMEM((entries, rows_dev), jnp.bfloat16)],
        ),
        name="select_rows",
    )(jnp.stack([first_wave, first_row]).astype(jnp.int32), row_map, legendre)


def legendre_kernel(*refs, parts, pots, patches):
    *table_refs, spectra_ref, out_ref = refs
    wave_count, entries, _ = table_refs[0].shape
    _, _, pair, level_count, _ = spectra_ref.shape
    half = level_count // pots
    width = pots * half
    groups = entries // (patches * SUB)
    lanes = groups * width
    rows = wave_count * pair
    rim = {}
    lane = lax.broadcasted_iota(jnp.int32, (1, lanes), 1)
    sub = lax.broadcasted_iota(jnp.int32, (rows, lanes), 0)
    for m in range(wave_count):
        table = table_refs[0][m]
        for other in table_refs[1:]:
            table = table + other[m]
        columns = [
            spectra_ref[e * pots + p, m, c, h * half : (h + 1) * half, :]
            for e in range(parts)
            for h in range(pots)
            for c in range(pair)
            for p in range(pots)
        ]
        product = dot_nt(table, jnp.concatenate(columns, axis=0))
        for e in range(parts):
            for h in range(pots):
                for c in range(pair):
                    base = ((e * pots + h) * pair + c) * width
                    tile = jnp.concatenate(
                        [
                            product[g * patches * SUB : (g + 1) * patches * SUB, base : base + width]
                            for g in range(groups)
                        ],
                        axis=1,
                    )
                    row = m * pair + c
                    for q in range(patches):
                        place = (e * patches + q) * pots + h
                        out_ref[place, row * SUB : (row + 1) * SUB, :] = tile[
                            q * SUB : (q + 1) * SUB
                        ].astype(jnp.bfloat16)
                        after = (q + 1) % patches
                        before = (q + patches - 1) % patches
                        edge = jnp.where(
                            lane < width,
                            tile[after * SUB : after * SUB + 1],
                            tile[before * SUB + SUB - 1 : before * SUB + SUB],
                        )
                        rim[place] = (
                            jnp.where(sub == row, edge, rim[place])
                            if place in rim
                            else jnp.broadcast_to(edge, (rows, lanes))
                        )
    for place, value in rim.items():
        out_ref[place, rows * SUB : rows * SUB + rows, :] = value.astype(jnp.bfloat16)


def legendre_rows(tables, spectra, parts, pots, patches):
    wave_count, entries, _ = tables[0].shape
    _, _, pair, level_count, _ = spectra.shape
    lanes = entries // (patches * SUB) * level_count
    rows = wave_count * pair
    return pl.pallas_call(
        functools.partial(legendre_kernel, parts=parts, pots=pots, patches=patches),
        out_shape=jax.ShapeDtypeStruct(
            (parts * patches * pots, rows * SUB + rows, lanes), jnp.bfloat16
        ),
        in_specs=[WHOLE] * (len(tables) + 1),
        out_specs=WHOLE,
        name="legendre_rows",
    )(*tables, spectra)


def lane_gather(values, index):
    return lax.gather(
        values,
        index[..., None],
        lax.GatherDimensionNumbers(
            offset_dims=(),
            collapsed_slice_dims=(1,),
            start_index_map=(1,),
            operand_batching_dims=(0,),
            start_indices_batching_dims=(0,),
        ),
        slice_sizes=(1, 1),
        mode="promise_in_bounds",
    )


def patch_kernel(
    own_ref, seg_ref, spectral_ref, fourier_ref, interp_ref, rims_ref, edges_ref, lengths_ref,
    out_ref, main_ref, rim_ref, cells_ref,
):
    sources, chunk, lanes = spectral_ref.shape
    rows = chunk // (SUB + 1)
    patches, blocks = seg_ref.shape
    groups = blocks // SUB
    width = lanes // groups
    half = out_ref.shape[0]
    pots = width // half
    tall = cells_ref.shape[0] // pots
    own = own_ref[0]
    for s in range(sources):
        main_ref[s * rows * SUB : (s + 1) * rows * SUB, :] = spectral_ref[s, : rows * SUB].astype(
            jnp.float32
        )
        rim_ref[s * rows : (s + 1) * rows, :] = spectral_ref[s, rows * SUB :].astype(jnp.float32)

    def block_cells(modes, segment, weights, position):
        grid = jnp.dot(modes, fourier_ref[segment], preferred_element_type=jnp.float32)
        cells = dot_nt(grid.astype(jnp.bfloat16), weights).astype(jnp.bfloat16)
        for p in range(pots):
            cells_ref[p * tall : p * tall + half, position : position + BLOCK] = cells[
                p * half : (p + 1) * half
            ]

    for s in range(SUB):
        modes = main_ref[pl.ds(s, sources * rows, stride=SUB), :].T.astype(jnp.bfloat16)
        for g in range(groups):
            b = g * SUB + s
            block_cells(
                modes[g * width : (g + 1) * width], seg_ref[own, b], interp_ref[b], HALO + b * BLOCK
            )
    modes = rim_ref[...].T.astype(jnp.bfloat16)
    before = lax.rem(own + patches - 1, patches)
    after = lax.rem(own + 1, patches)
    block_cells(
        modes[(groups - 1) * width :], seg_ref[before, blocks - 1], rims_ref[0], 0
    )
    block_cells(modes[:width], seg_ref[after, 0], rims_ref[1], HALO + blocks * BLOCK)

    extent = cells_ref.shape[1]

    def edge_chunk(step, carry):
        base = pl.multiple_of(step * LANE, LANE)
        at = []
        for column, pot in ((0, 1), (1, 1), (2, 0), (3, 0)):
            place = jnp.broadcast_to(edges_ref[pl.ds(column, 1), pl.ds(base, LANE)], (tall, LANE))
            high = (place >> 7).astype(jnp.int16)
            low = (place & (LANE - 1)).astype(jnp.int16)
            found = None
            for h in range(extent // LANE):
                part = lane_gather(
                    cells_ref[pot * tall : (pot + 1) * tall, h * LANE : (h + 1) * LANE], low
                )
                found = part if h == 0 else jnp.where(high == h, part, found)
            at.append(found.astype(jnp.float32))
        across = lengths_ref[pl.ds(0, 1), pl.ds(base, LANE)]
        along = lengths_ref[pl.ds(1, 1), pl.ds(base, LANE)]
        wind = (at[1] - at[0]) * across - (at[3] - at[2]) * along
        out_ref[:, pl.ds(base, LANE)] = wind[:half].astype(jnp.bfloat16)
        return carry

    lax.fori_loop(0, edges_ref.shape[1] // LANE, edge_chunk, 0)


def patch_winds(own, seg_map, spectral, fourier, interp, rims, edges, lengths, pots):
    sources, chunk, lanes = spectral.shape
    rows = chunk // (SUB + 1)
    _, blocks = seg_map.shape
    groups = blocks // SUB
    half = lanes // groups // pots
    tall = -(-half // 16) * 16
    extent = blocks * BLOCK + 2 * HALO
    return pl.pallas_call(
        patch_kernel,
        out_shape=jax.ShapeDtypeStruct((half, edges.shape[1]), jnp.bfloat16),
        in_specs=[SCALARS, SCALARS] + [WHOLE] * 6,
        out_specs=WHOLE,
        scratch_shapes=[
            pltpu.VMEM((sources * rows * SUB, lanes), jnp.float32),
            pltpu.VMEM((sources * rows, lanes), jnp.float32),
            pltpu.VMEM((pots * tall, extent), jnp.bfloat16),
        ],
        name="patch_winds",
    )(own, seg_map, spectral, fourier, interp, rims, edges, lengths)


def fourier_segments(parts, waves, pots, wave_count, own_waves):
    modes = parts * waves * pots * wave_count * 2
    shape = (NLON // BLOCK, modes, BLOCK)
    mode = lax.broadcasted_iota(jnp.int32, shape, 1)
    lon_index = lax.broadcasted_iota(jnp.int32, shape, 0) * BLOCK + lax.broadcasted_iota(
        jnp.int32, shape, 2
    )
    source = mode // (2 * wave_count)
    part_pot = source // (waves * pots) * pots + source % pots
    wave_index = (
        source // pots % waves * own_waves + part_pot * wave_count + mode // 2 % wave_count
    )
    angle_values = (wave_index * lon_index % NLON).astype(jnp.float32) * (2.0 * math.pi / NLON)
    factor = jnp.where(wave_index == 0, 1.0, 2.0).astype(jnp.float32)
    return jnp.where(
        mode % 2 == 0, factor * jnp.cos(angle_values), -factor * jnp.sin(angle_values)
    ).astype(jnp.bfloat16)


def body(spectra, legendre, row_map, seg_map, interp, edges, inv_len):
    parts, waves = lax.axis_size("ens"), lax.axis_size("wave")
    levs, pots = lax.axis_size("lev"), lax.axis_size("pot")
    own_spectra = spectra[0]
    own_waves, pair, level_count, degrees = own_spectra.shape
    shares = parts * pots
    wave_count = own_waves // shares
    share = lax.axis_index("ens") * pots + lax.axis_index("pot")
    own = lax.axis_index("wave")

    gathered = lax.all_to_all(
        own_spectra.reshape(shares, wave_count, pair, level_count, degrees),
        ("ens", "pot"),
        split_axis=0,
        concat_axis=0,
        tiled=True,
    )
    chosen = select_rows(
        legendre, row_map, share * wave_count, lax.axis_index("lev") * legendre.shape[1], wave_count
    )
    tables = [chosen] + [
        lax.ppermute(chosen, "lev", [(i, (i + s) % levs) for i in range(levs)])
        for s in range(1, levs)
    ]
    rims = jnp.stack(
        [
            lax.ppermute(interp[0, -1], "wave", [(i, (i + 1) % waves) for i in range(waves)]),
            lax.ppermute(interp[0, 0], "wave", [((i + 1) % waves, i) for i in range(waves)]),
        ]
    )
    outgoing = legendre_rows(tables, gathered, parts, pots, row_map.shape[0])
    incoming = lax.all_to_all(
        outgoing, ("ens", "wave", "pot"), split_axis=0, concat_axis=0, tiled=True
    )
    fourier = fourier_segments(parts, waves, pots, wave_count, own_waves)
    return patch_winds(
        own.reshape(1), seg_map, incoming, fourier, interp[0], rims, edges[0], inv_len[0], pots
    )


def solution(mesh):
    return jax.shard_map(
        body,
        mesh=mesh,
        in_specs=(
            P(("ens", "pot"), "wave", None, "lev", None),
            P("wave", "lev", None),
            P(),
            P(),
            P("wave", None, None, None),
            P("wave", None, None),
            P("wave", None, None),
        ),
        out_specs=P(("ens", "lev", "pot"), "wave"),
        check_vma=False,
    )
```

time: 375 us -> 73.8 us (0.20)
  local copies, waits for them, and re-layouts: 191 us -> 2.49 us
  waiting for transfers between devices: 117 us -> 15.1 us
  Pallas kernels: 0 us -> 34.5 us
  other arithmetic: 22.4 us -> 5.81 us
  matrix products: 15.2 us -> 0 us
  between operations: 13.6 us -> 0.05 us
    gather x4 -> x0, local copies, waits for them, and re-layouts: 94.3 us -> none  [the longest x1 43.3 us: body(): jnp.take(extended, first_cell, axis=1).astype(jnp.float32)]
    all_to_all x3 -> x2, waiting for transfers between devices: 72.3 us -> 11.2 us  [the longest x1 5.79 us: body(): lax.all_to_all(own_spectra.reshape(shares, wave_count, pair, level_count,...]
    reshape x5 -> x0, local copies, waits for them, and re-layouts: 56.2 us -> none  [the longest x2 55.9 us: body(): pieces = grid_field.reshape(level_count, rows_dev * segments, BLOCK)]
    pallas_call x0 -> x3, Pallas kernels: none -> 34.5 us  [the longest x1 26.9 us: patch_winds(): pl.pallas_call(patch_kernel, out_shape=jax.ShapeDtypeStruct((half, edges....]
    all_gather x1 -> x0, waiting for transfers between devices: 32.4 us -> none  [body(): lax.all_gather(own_spectra, 'lev', axis=2, tiled=True)]
    all_to_all x3 -> x0, local copies, waits for them, and re-layouts: 19.2 us -> none  [the longest x2 10.6 us: body(): lax.all_to_all(lax.all_to_all(spectral, 'lev', split_axis=0, concat_axis=...]
    unnamed x17 -> x6, local copies, waits for them, and re-layouts: 18.5 us -> 1.71 us
    dot_general x3 -> x0, matrix products: 15.2 us -> none  [the longest x1 9.14 us: body(): jnp.einsum('lrcm,cmk->lrk', banded, fourier_modes, preferred_element_type...]
  transfers between devices with their start and end apart: 7 -> 5, of which waited for: 7 -> 3; matrix products, arithmetic and copies ran while one was open for 2% -> 8% of each run, Pallas kernels for 0% -> 4%
where the time goes in v1:
time: 73.8 us; the launch traced here: 73.3 us
  Pallas kernels  34.5 us (47%)
  starting transfers between devices  15.3 us (21%)
  waiting for transfers between devices  15.1 us (20%)
  other arithmetic  5.81 us (8%)
  local copies, waits for them, and re-layouts  2.49 us (3%)
    pallas_call x1, Pallas kernels, patch_winds(): pl.pallas_call(patch_kernel, out_shape=jax.ShapeDtypeStruct((half, edges....  26.9 us
    all_to_all x1, waiting for transfers between devices, body(): lax.all_to_all(own_spectra.reshape(shares, wave_count, pair, level_count,...  5.79 us
    all_to_all x1, waiting for transfers between devices, body(): lax.all_to_all(outgoing, ('ens', 'wave', 'pot'), split_axis=0, concat_axi...  5.37 us
    all_to_all x1, starting transfers between devices, body(): lax.all_to_all(outgoing, ('ens', 'wave', 'pot'), split_axis=0, concat_axi...  4.98 us
    pallas_call x1, Pallas kernels, select_rows(): pl.pallas_call(select_kernel, out_shape=jax.ShapeDtypeStruct((wave_count,...  4.56 us
    convert_element_type x1, other arithmetic, fourier_segments(): return jnp.where(mode % 2 == 0, factor * jnp.cos(angle_values), -factor *...  4.52 us
    ppermute x1, waiting for transfers between devices, body(): lax.ppermute(chosen, 'lev', [(i, (i + s) % levs) for i in range(levs)])  3.94 us
    all_to_all x1, starting transfers between devices, body(): lax.all_to_all(own_spectra.reshape(shares, wave_count, pair, level_count,...  3.52 us
  transfers between devices with their start and end apart: 5, of which 3 were waited for; matrix products, arithmetic and copies ran while one was open for 8% of the time, Pallas kernels for 4%

profile of v1, /device:TPU:0, one launch (start us, length us, event | category | flops | bytes accessed | tf_op | source)
XLA Modules:
  0.0 73.3 jit_solution(4113374502088901658)
XLA Ops:
  0.0 0.6 pad_add_fusion.where_ref
  0.6 4.6 %select_rows.1.refs_0_ = bf16[4,128,512]{2,1,0:T(8,128)(2,1)} custom-call(s32[2]{0:T(128)} %pad_add_fusion.where_ref, s32[4,32]{1,0:T(4,128)} %rows_ref.1, bf16[16,384,512]{2,1,0:T(8,128)(2,1)} %legendre_ref.1), custom_call_target="tpu_custom_call" | custom-call | tf_op jit(solution)/shard_map/select_rows/pallas_call | solution.py:57
  5.2 3.0 %collective-permute-start = (bf16[4,128,512]{2,1,0:T(8,128)(2,1)}, bf16[4,128,512]{2,1,0:T(8,128)(2,1)S(1)}, u32[]{:S(2)}, u32[]{:S(2)}) collective-permute-start(bf16[4,128,512]{2,1,0:T(8,128)(2,1)} %select_rows.1.refs_0_), channel_id=1, source_target_pairs={{0,2},{2,0},{1,3},{3,1},{4,6},{6,4},{5,7},{7,5},{8,10},{10,8},{9,1... | collective-permute-start | bytes 1572872 | tf_op jit(solution)/shard_map/ppermute | solution.py:292
  8.2 3.5 %all-to-all-start = ((bf16[4,4,2,32,512]{4,3,2,1,0:T(8,128)(2,1)}), bf16[4,4,2,32,512]{4,3,2,1,0:T(8,128)(2,1)S(1)}, u32[]{:S(2)}, u32[]{:S(2)}) async-start(bf16[4,4,2,32,512]{4,3,2,1,0:T(8,128)(2,1)} %bitcast.3), calls=%async_computation | async-start | bytes 2097152 | tf_op jit(solution)/shard_map/all_to_all | solution.py:281
  11.7 0.8 %slice_bitcast_fusion.1 = (bf16[128,128]{1,0:T(8,128)(2,1)S(1)}, bf16[128,128]{1,0:T(8,128)(2,1)S(1)}) fusion(bf16[1,32,128,128]{3,2,1,0:T(8,128)(2,1)} %param.11), kind=kLoop, calls=%fused_computation.46 | loop fusion | bytes 131072 | tf_op jit(solution)/shard_map/squeeze | solution.py:297
  12.5 1.6 %collective-permute-start.1 = (bf16[128,128]{1,0:T(8,128)(2,1)S(1)}, bf16[128,128]{1,0:T(8,128)(2,1)S(1)}, u32[]{:S(2)}, u32[]{:S(2)}) collective-permute-start(bf16[128,128]{1,0:T(8,128)(2,1)S(1)} %get-tuple-element.5), channel_id=1, source_target_pairs={{0,4},{4,8},{8,12},{12,0},{1,5},{5,9},{9,13},{13,1},{2,6},{6,10},{... | collective-permute-start | bytes 98312 | tf_op jit(solution)/shard_map/ppermute | solution.py:297
  14.0 2.2 %collective-permute-start.2 = (bf16[128,128]{1,0:T(8,128)(2,1)S(1)}, bf16[128,128]{1,0:T(8,128)(2,1)S(1)}, u32[]{:S(2)}, u32[]{:S(2)}) collective-permute-start(bf16[128,128]{1,0:T(8,128)(2,1)S(1)} %get-tuple-element.6), channel_id=1, source_target_pairs={{4,0},{8,4},{12,8},{0,12},{5,1},{9,5},{13,9},{1,13},{6,2},{10,6},{... | collective-permute-start | bytes 98312 | tf_op jit(solution)/shard_map/ppermute | solution.py:298
  16.3 3.9 %collective-permute-done.refs_1_ = bf16[4,128,512]{2,1,0:T(8,128)(2,1)S(1)} collective-permute-done((bf16[4,128,512]{2,1,0:T(8,128)(2,1)}, bf16[4,128,512]{2,1,0:T(8,128)(2,1)S(1)}, u32[]{:S(2)}, u32[]{:S(2)}) %collective-permute-start) | collective-permute-done | bytes 524320 | tf_op jit(solution)/shard_map/ppermute | solution.py:292
  20.3 0.0 copy-start.2
  20.3 5.8 %all-to-all-done.refs_2_ = bf16[4,4,2,32,512]{4,3,2,1,0:T(8,128)(2,1)S(1)} async-done(((bf16[4,4,2,32,512]{4,3,2,1,0:T(8,128)(2,1)}), bf16[4,4,2,32,512]{4,3,2,1,0:T(8,128)(2,1)S(1)}, u32[]{:S(2)}, u32[]{:S(2)}) %all-to-all-start) | async-done | bytes 1048608 | tf_op jit(solution)/shard_map/all_to_all | solution.py:281
  26.1 0.0 copy-done.2
  26.1 0.0 copy-start
  26.1 1.0 %copy-done = bf16[4,4,2,32,512]{4,3,2,1,0:T(8,128)(2,1)} copy-done((bf16[4,4,2,32,512]{4,3,2,1,0:T(8,128)(2,1)}, bf16[4,4,2,32,512]{4,3,2,1,0:T(8,128)(2,1)S(1)}, u32[]{:S(2)}) %copy-start) | copy-done | bytes 1048600
  27.1 3.1 %legendre_rows.1 = bf16[16,72,128]{2,1,0:T(8,128)(2,1)} custom-call(bf16[4,128,512]{2,1,0:T(8,128)(2,1)} %select_rows.1.refs_0_, bf16[4,128,512]{2,1,0:T(8,128)(2,1)} %copy-done.2, bf16[4,4,2,32,512]{4,3,2,1,0:T(8,128)(2,1)} %copy-done), custom_call_target="tpu_custom_call" | custom-call | tf_op jit(solution)/shard_map/legendre_rows/pallas_call | solution.py:136
  30.1 5.0 %all-to-all-start.1 = ((bf16[16,72,128]{2,1,0:T(8,128)(2,1)}), bf16[16,72,128]{2,1,0:T(8,128)(2,1)S(1)}, u32[]{:S(2)}, u32[]{:S(2)}) async-start(bf16[16,72,128]{2,1,0:T(8,128)(2,1)} %legendre_rows.1), calls=%async_computation.1 | async-start | bytes 589824 | tf_op jit(solution)/shard_map/all_to_all | solution.py:302
  35.1 4.5 %fusion.1.fourier_ref = bf16[12,128,128]{2,1,0:T(8,128)(2,1)} fusion(s32[12]{0:T(128)S(1)} %iota_multiply_fusion, s32[128]{0:T(128)S(1)} %get-tuple-element.9, s32[128]{0:T(128)S(1)} %get-tuple-element.12, s32[128]{0:T(128)S(1)} %get-tuple-element.10, s32[128]{0:T(128)S(1)} %get-tuple-element.13, s32[128]{0:T(128)S(1)} %get-tuple-element.11, ...), kind=kLoop, calls=%fused_computation.23 | loop fusion | flops 15335424 | bytes 396720 | tf_op jit(solution)/shard_map/convert_element_type | solution.py:268
  39.6 0.0 collective-permute-done.1
  39.6 0.0 collective-permute-done.2
  39.7 0.6 pad_maximum_fusion.rims_ref
  40.3 5.4 %all-to-all-done.1.spectral_ref = bf16[16,72,128]{2,1,0:T(8,128)(2,1)S(1)} async-done(((bf16[16,72,128]{2,1,0:T(8,128)(2,1)}), bf16[16,72,128]{2,1,0:T(8,128)(2,1)S(1)}, u32[]{:S(2)}, u32[]{:S(2)}) %all-to-all-start.1) | async-done | bytes 294944 | tf_op jit(solution)/shard_map/all_to_all | solution.py:302
  45.7 0.0 copy-start.1
  45.7 0.7 copy-done.1
  46.4 26.9 %patch_winds.1 = bf16[16,12288]{1,0:T(8,128)(2,1)} custom-call(s32[1]{0:T(128)} %bitcast.own_ref, s32[4,32]{1,0:T(4,128)} %seg_ref.1, bf16[16,72,128]{2,1,0:T(8,128)(2,1)} %copy-done.1, bf16[12,128,128]{2,1,0:T(8,128)(2,1)} %fusion.1.fourier_ref, bf16[32,128,128]{2,1,0:T(8,128)(2,1)} %bitcast.13, bf16[2,128,128]{2,1,0:T(8,128)(2,1)} %pad_maximum_fusion.rims_ref, ...), custom_call_target="tpu_custom_call" | custom-call | tf_op jit(solution)/shard_map/patch_winds/pallas_call | solution.py:238
  (6 shorter events, 0.0 us)
Async XLA Ops:
  5.2 15.1 %collective-permute-start = (bf16[4,128,512]{2,1,0:T(8,128)(2,1)}, bf16[4,128,512]{2,1,0:T(8,128)(2,1)S(1)}, u32[]{:S(2)}, u32[]{:S(2)}) collective-permute-start(bf16[4,128,512]{2,1,0:T(8,128)(2,1)} %select_rows.1.refs_0_), channel_id=1, source_target_pairs={{0,2},{2,0},{1,3},{3,1},{4,6},{6,4},{5,7},{7,5},{8,10},{10,8},{9,1... | collective-permute-start | bytes 1572872 | tf_op jit(solution)/shard_map/ppermute | solution.py:292
  8.2 17.9 %all-to-all-start = ((bf16[4,4,2,32,512]{4,3,2,1,0:T(8,128)(2,1)}), bf16[4,4,2,32,512]{4,3,2,1,0:T(8,128)(2,1)S(1)}, u32[]{:S(2)}, u32[]{:S(2)}) async-start(bf16[4,4,2,32,512]{4,3,2,1,0:T(8,128)(2,1)} %bitcast.3), calls=%async_computation | async-start | bytes 2097152 | tf_op jit(solution)/shard_map/all_to_all | solution.py:281
  12.5 27.2 %collective-permute-start.1 = (bf16[128,128]{1,0:T(8,128)(2,1)S(1)}, bf16[128,128]{1,0:T(8,128)(2,1)S(1)}, u32[]{:S(2)}, u32[]{:S(2)}) collective-permute-start(bf16[128,128]{1,0:T(8,128)(2,1)S(1)} %get-tuple-element.5), channel_id=1, source_target_pairs={{0,4},{4,8},{8,12},{12,0},{1,5},{5,9},{9,13},{13,1},{2,6},{6,10},{... | collective-permute-start | bytes 98312 | tf_op jit(solution)/shard_map/ppermute | solution.py:297
  14.0 25.6 %collective-permute-start.2 = (bf16[128,128]{1,0:T(8,128)(2,1)S(1)}, bf16[128,128]{1,0:T(8,128)(2,1)S(1)}, u32[]{:S(2)}, u32[]{:S(2)}) collective-permute-start(bf16[128,128]{1,0:T(8,128)(2,1)S(1)} %get-tuple-element.6), channel_id=1, source_target_pairs={{4,0},{8,4},{12,8},{0,12},{5,1},{9,5},{13,9},{1,13},{6,2},{10,6},{... | collective-permute-start | bytes 98312 | tf_op jit(solution)/shard_map/ppermute | solution.py:298
  20.3 5.8 %copy-start.2 = (bf16[4,128,512]{2,1,0:T(8,128)(2,1)}, bf16[4,128,512]{2,1,0:T(8,128)(2,1)S(1)}, u32[]{:S(2)}) copy-start(bf16[4,128,512]{2,1,0:T(8,128)(2,1)S(1)} %collective-permute-done.refs_1_) | copy-start | bytes 1572868
  26.1 1.0 %copy-start = (bf16[4,4,2,32,512]{4,3,2,1,0:T(8,128)(2,1)}, bf16[4,4,2,32,512]{4,3,2,1,0:T(8,128)(2,1)S(1)}, u32[]{:S(2)}) copy-start(bf16[4,4,2,32,512]{4,3,2,1,0:T(8,128)(2,1)S(1)} %all-to-all-done.refs_2_) | copy-start | bytes 3145732
  30.1 15.5 %all-to-all-start.1 = ((bf16[16,72,128]{2,1,0:T(8,128)(2,1)}), bf16[16,72,128]{2,1,0:T(8,128)(2,1)S(1)}, u32[]{:S(2)}, u32[]{:S(2)}) async-start(bf16[16,72,128]{2,1,0:T(8,128)(2,1)} %legendre_rows.1), calls=%async_computation.1 | async-start | bytes 589824 | tf_op jit(solution)/shard_map/all_to_all | solution.py:302
  45.7 0.7 copy-start.1

commit v2 on v1

--- a/solution.py
+++ b/solution.py
@@ -13,7 +13,11 @@
 HALO = 128
 SUB = 8
 LANE = 128
+WINDOW = 2 * LANE
 WHOLE = pl.BlockSpec(memory_space=pltpu.VMEM)
+VMEM_ARRAY = 1 << 20
+PARAMS = pltpu.CompilerParams(vmem_limit_bytes=32 << 20)
+IN_HBM = pl.BlockSpec(memory_space=pltpu.HBM)
 SCALARS = pl.BlockSpec(memory_space=pltpu.SMEM)
 
 
@@ -21,54 +25,72 @@
     return lax.dot_general(a, b, (((1,), (1,)), ((), ())), preferred_element_type=jnp.float32)
 
 
-def select_kernel(where_ref, rows_ref, legendre_ref, out_ref, onehot_ref):
+def fits(shape, dtype):
+    return math.prod(shape) * jnp.dtype(dtype).itemsize <= VMEM_ARRAY
+
+
+def in_vmem(*arrays):
+    return [
+        pltpu.with_memory_space_constraint(x, pltpu.VMEM) if fits(x.shape, x.dtype) else x
+        for x in arrays
+    ]
+
+
+def result(shape, dtype):
+    return pltpu.VMEM(shape, dtype) if fits(shape, dtype) else jax.ShapeDtypeStruct(shape, dtype)
+
+
+def select_kernel(place_ref, map_ref, legendre_ref, out_ref, rows_ref, held_ref, sems):
     patches, blocks = rows_ref.shape
-    rows_dev = legendre_ref.shape[1]
-
-    @pl.when(pl.program_id(0) == 0)
-    def _():
-        first = where_ref[1]
-        eye = lax.broadcasted_iota(jnp.int32, (blocks, blocks), 0) == lax.broadcasted_iota(
-            jnp.int32, (blocks, blocks), 1
-        )
-        columns = []
-        for q in range(patches):
-            row = (rows_ref[q : q + 1, :] - first).astype(jnp.float32)
-            columns.append(jnp.sum(jnp.where(eye, row, 0.0), axis=1, keepdims=True))
-        lane = lax.broadcasted_iota(jnp.int32, (SUB, rows_dev), 1).astype(jnp.float32)
-        step = 0
-        for g in range(blocks // SUB):
-            for q in range(patches):
-                part = columns[q][g * SUB : (g + 1) * SUB]
-                onehot_ref[step * SUB : (step + 1) * SUB, :] = jnp.where(
-                    part == lane, 1.0, 0.0
-                ).astype(jnp.bfloat16)
-                step += 1
-
-    out_ref[0] = jnp.dot(
-        onehot_ref[...], legendre_ref[0], preferred_element_type=jnp.float32
-    ).astype(jnp.bfloat16)
-
-
-def select_rows(legendre, row_map, first_wave, first_row, wave_count):
+    wave_count, rows_dev, _ = held_ref.shape
+    copies = [
+        pltpu.make_async_copy(
+            legendre_ref.at[place_ref[0] * wave_count + m], held_ref.at[m], sems.at[m]
+        )
+        for m in range(wave_count)
+    ]
+    for copy in copies:
+        copy.start()
+    rows_copy = pltpu.make_async_copy(map_ref, rows_ref, sems.at[wave_count])
+    rows_copy.start()
+    rows_copy.wait()
+    first = place_ref[1] * rows_dev
+    eye = lax.broadcasted_iota(jnp.int32, (blocks, blocks), 0) == lax.broadcasted_iota(
+        jnp.int32, (blocks, blocks), 1
+    )
+    columns = []
+    for q in range(patches):
+        row = (rows_ref[q : q + 1, :] - first).astype(jnp.float32)
+        columns.append(jnp.sum(jnp.where(eye, row, 0.0), axis=1, keepdims=True))
+    order = jnp.concatenate(
+        [columns[q][g * SUB : (g + 1) * SUB] for g in range(blocks // SUB) for q in range(patches)],
+        axis=0,
+    )
+    lane = lax.broadcasted_iota(jnp.int32, (patches * blocks, rows_dev), 1).astype(jnp.float32)
+    onehot = jnp.where(order == lane, 1.0, 0.0).astype(jnp.bfloat16)
+    for m in range(wave_count):
+        copies[m].wait()
+        out_ref[m] = jnp.dot(onehot, held_ref[m], preferred_element_type=jnp.float32).astype(
+            jnp.bfloat16
+        )
+
+
+def select_rows(place, row_map, legendre, wave_count):
     _, rows_dev, degrees = legendre.shape
     patches, blocks = row_map.shape
-    entries = patches * blocks
     return pl.pallas_call(
         select_kernel,
-        out_shape=jax.ShapeDtypeStruct((wave_count, entries, degrees), jnp.bfloat16),
-        grid_spec=pltpu.PrefetchScalarGridSpec(
-            num_scalar_prefetch=1,
-            grid=(wave_count,),
-            in_specs=[
-                pl.BlockSpec((patches, blocks), lambda i, where: (0, 0)),
-                pl.BlockSpec((1, rows_dev, degrees), lambda i, where: (where[0] + i, 0, 0)),
-            ],
-            out_specs=pl.BlockSpec((1, entries, degrees), lambda i, where: (i, 0, 0)),
-            scratch_shapes=[pltpu.VMEM((entries, rows_dev), jnp.bfloat16)],
-        ),
+        out_shape=result((wave_count, patches * blocks, degrees), jnp.bfloat16),
+        in_specs=[SCALARS, IN_HBM, IN_HBM],
+        out_specs=WHOLE,
+        scratch_shapes=[
+            pltpu.VMEM((patches, blocks), jnp.int32),
+            pltpu.VMEM((wave_count, rows_dev, degrees), jnp.bfloat16),
+            pltpu.SemaphoreType.DMA((wave_count + 1,)),
+        ],
+        compiler_params=PARAMS,
         name="select_rows",
-    )(jnp.stack([first_wave, first_row]).astype(jnp.int32), row_map, legendre)
+    )(place, *(pltpu.with_memory_space_constraint(x, pltpu.HBM) for x in (row_map, legendre)))
 
 
 def legendre_kernel(*refs, parts, pots, patches):
@@ -135,13 +157,12 @@
     rows = wave_count * pair
     return pl.pallas_call(
         functools.partial(legendre_kernel, parts=parts, pots=pots, patches=patches),
-        out_shape=jax.ShapeDtypeStruct(
-            (parts * patches * pots, rows * SUB + rows, lanes), jnp.bfloat16
-        ),
+        out_shape=result((parts * patches * pots, rows * SUB + rows, lanes), jnp.bfloat16),
         in_specs=[WHOLE] * (len(tables) + 1),
         out_specs=WHOLE,
+        compiler_params=PARAMS,
         name="legendre_rows",
-    )(*tables, spectra)
+    )(*in_vmem(*tables, spectra))
 
 
 def lane_gather(values, index):
@@ -160,9 +181,56 @@
     )
 
 
+def windowed_edges(tables_ref, edges_ref, base, count, tall, windows):
+    ends = [edges_ref[pl.ds(k, 1), pl.ds(base, count)] for k in range(4)]
+    window = (ends[0] - HALO) // WINDOW
+    ends = [end - window * WINDOW for end in ends]
+    cell = lax.broadcasted_iota(jnp.int16, (2 * WINDOW, count), 0)
+    here = jnp.broadcast_to(window, (SUB, count))
+    sums = []
+    for pot, plus, minus in ((1, 1, 0), (0, 3, 2)):
+        one = jnp.where(ends[plus] == ends[minus], 0.0, 1.0).astype(jnp.bfloat16)
+        at = [
+            jnp.broadcast_to(ends[k], (2 * SUB, count)).astype(jnp.int16)[:1]
+            for k in (plus, minus)
+        ]
+        signs = jnp.where(
+            cell == at[0], one, jnp.where(cell == at[1], jnp.bfloat16(-1), jnp.bfloat16(0))
+        )
+        every = jnp.dot(
+            tables_ref[pot, : windows * tall, :], signs[:WINDOW], preferred_element_type=jnp.float32
+        ) + jnp.dot(
+            tables_ref[pot, tall:, :], signs[WINDOW:], preferred_element_type=jnp.float32
+        )
+        found = [every[s * SUB : (s + 1) * SUB] for s in range(tall // SUB)]
+        for h in range(1, windows):
+            for s in range(tall // SUB):
+                row = h * tall + s * SUB
+                found[s] = jnp.where(here == h, every[row : row + SUB], found[s])
+        sums.append(jnp.concatenate(found, axis=0))
+    return sums
+
+
+def gathered_edges(cells_ref, edges_ref, base, tall):
+    extent = cells_ref.shape[1]
+    at = []
+    for column, pot in ((0, 1), (1, 1), (2, 0), (3, 0)):
+        place = jnp.broadcast_to(edges_ref[pl.ds(column, 1), pl.ds(base, LANE)], (tall, LANE))
+        high = (place >> 7).astype(jnp.int16)
+        low = (place & (LANE - 1)).astype(jnp.int16)
+        found = None
+        for h in range(extent // LANE):
+            part = lane_gather(
+                cells_ref[pot * tall : (pot + 1) * tall, h * LANE : (h + 1) * LANE], low
+            )
+            found = part if h == 0 else jnp.where(high == h, part, found)
+        at.append(found.astype(jnp.float32))
+    return [at[1] - at[0], at[3] - at[2]]
+
+
 def patch_kernel(
-    own_ref, seg_ref, spectral_ref, fourier_ref, interp_ref, rims_ref, edges_ref, lengths_ref,
-    out_ref, main_ref, rim_ref, cells_ref,
+    place_ref, seg_ref, spectral_ref, fourier_ref, interp_ref, before_ref, after_ref, edges_ref,
+    lengths_ref, out_ref, main_ref, rim_ref, cells_ref, tables_ref,
 ):
     sources, chunk, lanes = spectral_ref.shape
     rows = chunk // (SUB + 1)
@@ -170,9 +238,10 @@
     groups = blocks // SUB
     width = lanes // groups
     half = out_ref.shape[0]
-    pots = width // half
+    pots, _, _ = tables_ref.shape
     tall = cells_ref.shape[0] // pots
-    own = own_ref[0]
+    windows = blocks * BLOCK // WINDOW
+    own = place_ref[2]
     for s in range(sources):
         main_ref[s * rows * SUB : (s + 1) * rows * SUB, :] = spectral_ref[s, : rows * SUB].astype(
             jnp.float32
@@ -182,10 +251,12 @@
     def block_cells(modes, segment, weights, position):
         grid = jnp.dot(modes, fourier_ref[segment], preferred_element_type=jnp.float32)
         cells = dot_nt(grid.astype(jnp.bfloat16), weights).astype(jnp.bfloat16)
+        row = position // WINDOW * tall
+        column = position % WINDOW
         for p in range(pots):
-            cells_ref[p * tall : p * tall + half, position : position + BLOCK] = cells[
-                p * half : (p + 1) * half
-            ]
+            part = cells[p * half : (p + 1) * half]
+            cells_ref[p * tall : p * tall + half, position : position + BLOCK] = part
+            tables_ref[p, row : row + half, column : column + BLOCK] = part
 
     for s in range(SUB):
         modes = main_ref[pl.ds(s, sources * rows, stride=SUB), :].T.astype(jnp.bfloat16)
@@ -197,56 +268,56 @@
     modes = rim_ref[...].T.astype(jnp.bfloat16)
     before = lax.rem(own + patches - 1, patches)
     after = lax.rem(own + 1, patches)
-    block_cells(
-        modes[(groups - 1) * width :], seg_ref[before, blocks - 1], rims_ref[0], 0
-    )
-    block_cells(modes[:width], seg_ref[after, 0], rims_ref[1], HALO + blocks * BLOCK)
-
-    extent = cells_ref.shape[1]
+    block_cells(modes[(groups - 1) * width :], seg_ref[before, blocks - 1], before_ref[...], 0)
+    block_cells(modes[:width], seg_ref[after, 0], after_ref[...], HALO + blocks * BLOCK)
+
+    def finish(sums, base, count):
+        across = lengths_ref[pl.ds(0, 1), pl.ds(base, count)]
+        along = lengths_ref[pl.ds(1, 1), pl.ds(base, count)]
+        wind = sums[0] * across - sums[1] * along
+        out_ref[:, pl.ds(base, count)] = wind[:half].astype(jnp.bfloat16)
+
+    span = WINDOW + LANE
+    total = edges_ref.shape[1]
+    assert total % span == 0
+    spans = total // span
+    repeat = math.gcd(spans, 4)
 
     def edge_chunk(step, carry):
-        base = pl.multiple_of(step * LANE, LANE)
-        at = []
-        for column, pot in ((0, 1), (1, 1), (2, 0), (3, 0)):
-            place = jnp.broadcast_to(edges_ref[pl.ds(column, 1), pl.ds(base, LANE)], (tall, LANE))
-            high = (place >> 7).astype(jnp.int16)
-            low = (place & (LANE - 1)).astype(jnp.int16)
-            found = None
-            for h in range(extent // LANE):
-                part = lane_gather(
-                    cells_ref[pot * tall : (pot + 1) * tall, h * LANE : (h + 1) * LANE], low
-                )
-                found = part if h == 0 else jnp.where(high == h, part, found)
-            at.append(found.astype(jnp.float32))
-        across = lengths_ref[pl.ds(0, 1), pl.ds(base, LANE)]
-        along = lengths_ref[pl.ds(1, 1), pl.ds(base, LANE)]
-        wind = (at[1] - at[0]) * across - (at[3] - at[2]) * along
-        out_ref[:, pl.ds(base, LANE)] = wind[:half].astype(jnp.bfloat16)
+        for k in range(repeat):
+            base = pl.multiple_of((step * repeat + k) * span, LANE)
+            finish(
+                windowed_edges(tables_ref, edges_ref, base, WINDOW, tall, windows), base, WINDOW
+            )
+            base = pl.multiple_of(base + WINDOW, LANE)
+            finish(gathered_edges(cells_ref, edges_ref, base, tall), base, LANE)
         return carry
 
-    lax.fori_loop(0, edges_ref.shape[1] // LANE, edge_chunk, 0)
-
-
-def patch_winds(own, seg_map, spectral, fourier, interp, rims, edges, lengths, pots):
+    lax.fori_loop(0, spans // repeat, edge_chunk, 0)
+
+
+def patch_winds(place, seg_map, spectral, fourier, interp, before, after, edges, lengths, pots):
     sources, chunk, lanes = spectral.shape
     rows = chunk // (SUB + 1)
     _, blocks = seg_map.shape
     groups = blocks // SUB
     half = lanes // groups // pots
-    tall = -(-half // 16) * 16
+    tall = -(-half // (2 * SUB)) * 2 * SUB
     extent = blocks * BLOCK + 2 * HALO
     return pl.pallas_call(
         patch_kernel,
         out_shape=jax.ShapeDtypeStruct((half, edges.shape[1]), jnp.bfloat16),
-        in_specs=[SCALARS, SCALARS] + [WHOLE] * 6,
+        in_specs=[SCALARS, SCALARS] + [WHOLE] * 7,
         out_specs=WHOLE,
         scratch_shapes=[
             pltpu.VMEM((sources * rows * SUB, lanes), jnp.float32),
             pltpu.VMEM((sources * rows, lanes), jnp.float32),
             pltpu.VMEM((pots * tall, extent), jnp.bfloat16),
+            pltpu.VMEM((pots, extent // WINDOW * tall, WINDOW), jnp.bfloat16),
         ],
+        compiler_params=PARAMS,
         name="patch_winds",
-    )(own, seg_map, spectral, fourier, interp, rims, edges, lengths)
+    )(place, seg_map, *in_vmem(spectral, fourier, interp, before, after, edges, lengths))
 
 
 def fourier_segments(parts, waves, pots, wave_count, own_waves):
@@ -278,6 +349,7 @@
     share = lax.axis_index("ens") * pots + lax.axis_index("pot")
     own = lax.axis_index("wave")
 
+    place = jnp.stack([share, lax.axis_index("lev"), own]).astype(jnp.int32)
     gathered = lax.all_to_all(
         own_spectra.reshape(shares, wave_count, pair, level_count, degrees),
         ("ens", "pot"),
@@ -285,26 +357,20 @@
         concat_axis=0,
         tiled=True,
     )
-    chosen = select_rows(
-        legendre, row_map, share * wave_count, lax.axis_index("lev") * legendre.shape[1], wave_count
-    )
+    chosen = select_rows(place, row_map, legendre, wave_count)
     tables = [chosen] + [
         lax.ppermute(chosen, "lev", [(i, (i + s) % levs) for i in range(levs)])
         for s in range(1, levs)
     ]
-    rims = jnp.stack(
-        [
-            lax.ppermute(interp[0, -1], "wave", [(i, (i + 1) % waves) for i in range(waves)]),
-            lax.ppermute(interp[0, 0], "wave", [((i + 1) % waves, i) for i in range(waves)]),
-        ]
-    )
+    before = lax.ppermute(interp[0, -1], "wave", [(i, (i + 1) % waves) for i in range(waves)])
+    after = lax.ppermute(interp[0, 0], "wave", [((i + 1) % waves, i) for i in range(waves)])
     outgoing = legendre_rows(tables, gathered, parts, pots, row_map.shape[0])
     incoming = lax.all_to_all(
         outgoing, ("ens", "wave", "pot"), split_axis=0, concat_axis=0, tiled=True
     )
     fourier = fourier_segments(parts, waves, pots, wave_count, own_waves)
     return patch_winds(
-        own.reshape(1), seg_map, incoming, fourier, interp[0], rims, edges[0], inv_len[0], pots
+        place, seg_map, incoming, fourier, interp[0], before, after, edges[0], inv_len[0], pots
     )
 
 

time: 73.8 us -> 51.3 us (0.70)
  Pallas kernels: 34.5 us -> 14.4 us
  local copies, waits for them, and re-layouts: 2.49 us -> 0.62 us
  waiting for transfers between devices: 15.1 us -> 13.5 us
  other arithmetic: 5.81 us -> 7.04 us
    pallas_call x1, Pallas kernels: 26.9 us -> 9.99 us  [patch_winds(): pl.pallas_call(patch_kernel, out_shape=jax.ShapeDtypeStruct((half, edges....]
    ppermute x1, waiting for transfers between devices: 3.94 us -> 1.23 us  [body(): lax.ppermute(chosen, 'lev', [(i, (i + s) % levs) for i in range(levs)])]
    pallas_call x1, Pallas kernels: 4.56 us -> 2.86 us  [select_rows(): pl.pallas_call(select_kernel, out_shape=result((wave_count, patches * blo...]
    unnamed x6 -> x8, local copies, waits for them, and re-layouts: 1.71 us -> 0.01 us
    pallas_call x1, Pallas kernels: 3.08 us -> 1.53 us  [legendre_rows(): pl.pallas_call(functools.partial(legendre_kernel, parts=parts, pots=pots,...]
    another operation x2 -> x1, other arithmetic: 1.26 us -> 0.08 us  [body(): place = jnp.stack([share, lax.axis_index('lev'), own]).astype(jnp.int32)]
    all_to_all x1, waiting for transfers between devices: 5.37 us -> 6.29 us  [body(): lax.all_to_all(outgoing, ('ens', 'wave', 'pot'), split_axis=0, concat_axi...]
  transfers between devices with their start and end apart: 5 -> 5, of which waited for: 3 -> 3; matrix products, arithmetic and copies ran while one was open for 8% -> 15% of each run, Pallas kernels for 4% -> 3%
where the time goes in v2:
time: 51.3 us; the launch traced here: 51 us
  starting transfers between devices  15.4 us (30%)
  Pallas kernels  14.4 us (28%)
  waiting for transfers between devices  13.5 us (26%)
  other arithmetic  7.04 us (14%)
  local copies, waits for them, and re-layouts  0.62 us (1%)
    pallas_call x1, Pallas kernels, patch_winds(): pl.pallas_call(patch_kernel, out_shape=jax.ShapeDtypeStruct((half, edges....  9.99 us
    all_to_all x1, waiting for transfers between devices, body(): lax.all_to_all(outgoing, ('ens', 'wave', 'pot'), split_axis=0, concat_axi...  6.29 us
    all_to_all x1, waiting for transfers between devices, body(): lax.all_to_all(own_spectra.reshape(shares, wave_count, pair, level_count,...  5.99 us
    all_to_all x1, starting transfers between devices, body(): lax.all_to_all(outgoing, ('ens', 'wave', 'pot'), split_axis=0, concat_axi...  4.99 us
    convert_element_type x1, other arithmetic, fourier_segments(): return jnp.where(mode % 2 == 0, factor * jnp.cos(angle_values), -factor *...  4.23 us
    all_to_all x1, starting transfers between devices, body(): lax.all_to_all(own_spectra.reshape(shares, wave_count, pair, level_count,...  3.52 us
    ppermute x1, starting transfers between devices, body(): lax.ppermute(chosen, 'lev', [(i, (i + s) % levs) for i in range(levs)])  3.04 us
    pallas_call x1, Pallas kernels, select_rows(): pl.pallas_call(select_kernel, out_shape=result((wave_count, patches * blo...  2.86 us
  transfers between devices with their start and end apart: 5, of which 3 were waited for; matrix products, arithmetic and copies ran while one was open for 15% of the time, Pallas kernels for 3%

profile of v2, /device:TPU:0, one launch (start us, length us, event | category | flops | bytes accessed | tf_op | source)
XLA Modules:
  0.0 51.0 jit_solution(5819853238111153065)
XLA Ops:
  0.0 0.1 pad_add_fusion.place_ref
  0.1 2.9 %select_rows.1.refs_0_ = bf16[4,128,512]{2,1,0:T(8,128)(2,1)S(1)} custom-call(s32[3]{0:T(128)S(1)} %pad_add_fusion.place_ref, s32[4,32]{1,0:T(4,128)} %map_ref.1, bf16[16,384,512]{2,1,0:T(8,128)(2,1)} %legendre_ref.1), custom_call_target="tpu_custom_call" | custom-call | tf_op jit(solution)/shard_map/select_rows/pallas_call | solution.py:81
  3.0 3.0 %collective-permute-start = (bf16[4,128,512]{2,1,0:T(8,128)(2,1)S(1)}, bf16[4,128,512]{2,1,0:T(8,128)(2,1)S(1)}, u32[]{:S(2)}, u32[]{:S(2)}) collective-permute-start(bf16[4,128,512]{2,1,0:T(8,128)(2,1)S(1)} %select_rows.1.refs_0_), channel_id=1, source_target_pairs={{0,2},{2,0},{1,3},{3,1},{4,6},{6,4},{5,7},{7,5},{8,10},{10,8},{9,1... | collective-permute-start | bytes 1572872 | tf_op jit(solution)/shard_map/ppermute | solution.py:362
  6.0 3.5 %all-to-all-start = ((bf16[4,4,2,32,512]{4,3,2,1,0:T(8,128)(2,1)}), bf16[4,4,2,32,512]{4,3,2,1,0:T(8,128)(2,1)S(1)}, u32[]{:S(2)}, u32[]{:S(2)}) async-start(bf16[4,4,2,32,512]{4,3,2,1,0:T(8,128)(2,1)} %bitcast.14), calls=%async_computation | async-start | bytes 2097152 | tf_op jit(solution)/shard_map/all_to_all | solution.py:353
  9.5 0.0 copy-done
  9.5 0.6 %slice_bitcast_fusion = (bf16[128,128]{1,0:T(8,128)(2,1)S(1)}, bf16[128,128]{1,0:T(8,128)(2,1)}) fusion(bf16[1,32,128,128]{3,2,1,0:T(8,128)(2,1)S(1)} %copy-done), kind=kLoop, calls=%fused_computation.44 | loop fusion | bytes 131072 | tf_op jit(solution)/shard_map/squeeze | solution.py:366
  10.1 1.6 %collective-permute-start.1 = (bf16[128,128]{1,0:T(8,128)(2,1)}, bf16[128,128]{1,0:T(8,128)(2,1)S(1)}, u32[]{:S(2)}, u32[]{:S(2)}) collective-permute-start(bf16[128,128]{1,0:T(8,128)(2,1)} %get-tuple-element.6), channel_id=1, source_target_pairs={{0,4},{4,8},{8,12},{12,0},{1,5},{5,9},{9,13},{13,1},{2,6},{6,10},{... | collective-permute-start | bytes 98312 | tf_op jit(solution)/shard_map/ppermute | solution.py:365
  11.7 2.2 %collective-permute-start.2 = (bf16[128,128]{1,0:T(8,128)(2,1)S(1)}, bf16[128,128]{1,0:T(8,128)(2,1)S(1)}, u32[]{:S(2)}, u32[]{:S(2)}) collective-permute-start(bf16[128,128]{1,0:T(8,128)(2,1)S(1)} %get-tuple-element.5), channel_id=1, source_target_pairs={{4,0},{8,4},{12,8},{0,12},{5,1},{9,5},{13,9},{1,13},{6,2},{10,6},{... | collective-permute-start | bytes 98312 | tf_op jit(solution)/shard_map/ppermute | solution.py:366
  14.0 0.6 %compare_and_fusion.2 = pred[128]{0:T(512)(128)(4,1)} fusion(), kind=kLoop, calls=%fused_computation.53 | loop fusion | flops 640 | bytes 128 | tf_op jit(solution)/shard_map/jit(floor_divide)/and | solution.py:333
  14.5 0.5 iota_multiply_fusion
  15.0 0.6 %iota_and_fusion.1 = (s32[128]{0:T(128)}, s32[128]{0:T(128)}) fusion(), kind=kLoop, calls=%fused_computation.52 | loop fusion | flops 384 | bytes 1024 | tf_op jit(solution)/shard_map/jit(remainder)/rem | solution.py:338
  15.6 0.5 %broadcast_add_fusion.1 = (s32[128]{0:T(128)}, s32[128]{0:T(128)}) fusion(), kind=kLoop, calls=%fused_computation.57 | loop fusion | flops 512 | bytes 1024 | tf_op jit(solution)/shard_map/jit(floor_divide)/sub | solution.py:330
  16.1 0.6 %compare_and_fusion = (pred[128]{0:T(512)(128)(4,1)}, pred[128]{0:T(512)(128)(4,1)}) fusion(), kind=kLoop, calls=%fused_computation.46 | loop fusion | flops 1152 | bytes 256 | tf_op jit(solution)/shard_map/jit(floor_divide)/and | solution.py:330
  16.7 1.2 %collective-permute-done.refs_1_ = bf16[4,128,512]{2,1,0:T(8,128)(2,1)S(1)} collective-permute-done((bf16[4,128,512]{2,1,0:T(8,128)(2,1)S(1)}, bf16[4,128,512]{2,1,0:T(8,128)(2,1)S(1)}, u32[]{:S(2)}, u32[]{:S(2)}) %collective-permute-start) | collective-permute-done | bytes 524320 | tf_op jit(solution)/shard_map/ppermute | solution.py:362
  17.9 6.0 %all-to-all-done.refs_2_ = bf16[4,4,2,32,512]{4,3,2,1,0:T(8,128)(2,1)S(1)} async-done(((bf16[4,4,2,32,512]{4,3,2,1,0:T(8,128)(2,1)}), bf16[4,4,2,32,512]{4,3,2,1,0:T(8,128)(2,1)S(1)}, u32[]{:S(2)}, u32[]{:S(2)}) %all-to-all-start) | async-done | bytes 1048608 | tf_op jit(solution)/shard_map/all_to_all | solution.py:353
  23.9 1.5 %legendre_rows.1 = bf16[16,72,128]{2,1,0:T(8,128)(2,1)} custom-call(bf16[4,128,512]{2,1,0:T(8,128)(2,1)S(1)} %select_rows.1.refs_0_, bf16[4,128,512]{2,1,0:T(8,128)(2,1)S(1)} %collective-permute-done.refs_1_, bf16[4,4,2,32,512]{4,3,2,1,0:T(8,128)(2,1)S(1)} %all-to-all-done.refs_2_), custom_call_target="tpu_custom_call" | custom-call | tf_op jit(solution)/shard_map/legendre_rows/pallas_call | solution.py:158
  25.4 5.0 %all-to-all-start.1 = ((bf16[16,72,128]{2,1,0:T(8,128)(2,1)}), bf16[16,72,128]{2,1,0:T(8,128)(2,1)S(1)}, u32[]{:S(2)}, u32[]{:S(2)}) async-start(bf16[16,72,128]{2,1,0:T(8,128)(2,1)} %legendre_rows.1), calls=%async_computation.1 | async-start | bytes 589824 | tf_op jit(solution)/shard_map/all_to_all | solution.py:368
  30.4 4.2 %fusion.1.fourier_ref = bf16[12,128,128]{2,1,0:T(8,128)(2,1)S(1)} fusion(s32[12]{0:T(128)} %iota_multiply_fusion, s32[128]{0:T(128)S(1)} %get-tuple-element.9, s32[128]{0:T(128)} %get-tuple-element.12, s32[128]{0:T(128)S(1)} %get-tuple-element.10, s32[128]{0:T(128)} %get-tuple-element.13, s32[128]{0:T(128)} %get-tuple-element.11, s32[128]{0:T(128)} %get-tuple-element.14, ...), kind=kLoop, calls=%fused_computation.23 | loop fusion | flops 15335424 | bytes 396720 | tf_op jit(solution)/shard_map/convert_element_type | solution.py:339
  34.7 0.0 collective-permute-done.1.before_ref
  34.7 0.0 collective-permute-done.2.after_ref
  34.7 6.3 %all-to-all-done.1.spectral_ref = bf16[16,72,128]{2,1,0:T(8,128)(2,1)S(1)} async-done(((bf16[16,72,128]{2,1,0:T(8,128)(2,1)}), bf16[16,72,128]{2,1,0:T(8,128)(2,1)S(1)}, u32[]{:S(2)}, u32[]{:S(2)}) %all-to-all-start.1) | async-done | bytes 294944 | tf_op jit(solution)/shard_map/all_to_all | solution.py:368
  41.0 0.0 copy-done.1
  41.0 0.0 copy-done.2
  41.0 10.0 %patch_winds.1 = bf16[16,12288]{1,0:T(8,128)(2,1)} custom-call(s32[3]{0:T(128)S(1)} %pad_add_fusion.place_ref, s32[4,32]{1,0:T(4,128)S(1)} %copy-done.3, bf16[16,72,128]{2,1,0:T(8,128)(2,1)S(1)} %all-to-all-done.1.spectral_ref, bf16[12,128,128]{2,1,0:T(8,128)(2,1)S(1)} %fusion.1.fourier_ref, bf16[32,128,128]{2,1,0:T(8,128)(2,1)S(1)} %bitcast.11, ...), custom_call_target="tpu_custom_call" | custom-call | tf_op jit(solution)/shard_map/patch_winds/pallas_call | solution.py:307
  (6 shorter events, 0.0 us)
Async XLA Ops:
  0.0 9.5 %copy-start = (bf16[1,32,128,128]{3,2,1,0:T(8,128)(2,1)S(1)}, bf16[1,32,128,128]{3,2,1,0:T(8,128)(2,1)}, u32[]{:S(2)}) copy-start(bf16[1,32,128,128]{3,2,1,0:T(8,128)(2,1)} %param.11) | copy-start | bytes 3145732
  0.1 40.9 %copy-start.1 = (s32[1,4,12288]{2,1,0:T(4,128)S(1)}, s32[1,4,12288]{2,1,0:T(4,128)}, u32[]{:S(2)}) copy-start(s32[1,4,12288]{2,1,0:T(4,128)} %param.12) | copy-start | bytes 589828
  0.1 40.9 %copy-start.2 = (f32[1,2,12288]{2,1,0:T(2,128)S(1)}, f32[1,2,12288]{2,1,0:T(2,128)}, u32[]{:S(2)}) copy-start(f32[1,2,12288]{2,1,0:T(2,128)} %param.13) | copy-start | bytes 294916
  0.1 40.9 %copy-start.3 = (s32[4,32]{1,0:T(4,128)S(1)}, s32[4,32]{1,0:T(4,128)}, u32[]{:S(2)}) copy-start(s32[4,32]{1,0:T(4,128)} %seg_ref.1) | copy-start | bytes 1540
  3.0 15.0 %collective-permute-start = (bf16[4,128,512]{2,1,0:T(8,128)(2,1)S(1)}, bf16[4,128,512]{2,1,0:T(8,128)(2,1)S(1)}, u32[]{:S(2)}, u32[]{:S(2)}) collective-permute-start(bf16[4,128,512]{2,1,0:T(8,128)(2,1)S(1)} %select_rows.1.refs_0_), channel_id=1, source_target_pairs={{0,2},{2,0},{1,3},{3,1},{4,6},{6,4},{5,7},{7,5},{8,10},{10,8},{9,1... | collective-permute-start | bytes 1572872 | tf_op jit(solution)/shard_map/ppermute | solution.py:362
  6.0 17.9 %all-to-all-start = ((bf16[4,4,2,32,512]{4,3,2,1,0:T(8,128)(2,1)}), bf16[4,4,2,32,512]{4,3,2,1,0:T(8,128)(2,1)S(1)}, u32[]{:S(2)}, u32[]{:S(2)}) async-start(bf16[4,4,2,32,512]{4,3,2,1,0:T(8,128)(2,1)} %bitcast.14), calls=%async_computation | async-start | bytes 2097152 | tf_op jit(solution)/shard_map/all_to_all | solution.py:353
  10.1 24.5 %collective-permute-start.1 = (bf16[128,128]{1,0:T(8,128)(2,1)}, bf16[128,128]{1,0:T(8,128)(2,1)S(1)}, u32[]{:S(2)}, u32[]{:S(2)}) collective-permute-start(bf16[128,128]{1,0:T(8,128)(2,1)} %get-tuple-element.6), channel_id=1, source_target_pairs={{0,4},{4,8},{8,12},{12,0},{1,5},{5,9},{9,13},{13,1},{2,6},{6,10},{... | collective-permute-start | bytes 98312 | tf_op jit(solution)/shard_map/ppermute | solution.py:365
  11.7 23.0 %collective-permute-start.2 = (bf16[128,128]{1,0:T(8,128)(2,1)S(1)}, bf16[128,128]{1,0:T(8,128)(2,1)S(1)}, u32[]{:S(2)}, u32[]{:S(2)}) collective-permute-start(bf16[128,128]{1,0:T(8,128)(2,1)S(1)} %get-tuple-element.5), channel_id=1, source_target_pairs={{4,0},{8,4},{12,8},{0,12},{5,1},{9,5},{13,9},{1,13},{6,2},{10,6},{... | collective-permute-start | bytes 98312 | tf_op jit(solution)/shard_map/ppermute | solution.py:366
  25.4 15.5 %all-to-all-start.1 = ((bf16[16,72,128]{2,1,0:T(8,128)(2,1)}), bf16[16,72,128]{2,1,0:T(8,128)(2,1)S(1)}, u32[]{:S(2)}, u32[]{:S(2)}) async-start(bf16[16,72,128]{2,1,0:T(8,128)(2,1)} %legendre_rows.1), calls=%async_computation.1 | async-start | bytes 589824 | tf_op jit(solution)/shard_map/all_to_all | solution.py:368

commit v3 on v2

--- a/solution.py
+++ b/solution.py
@@ -93,15 +93,17 @@
     )(place, *(pltpu.with_memory_space_constraint(x, pltpu.HBM) for x in (row_map, legendre)))
 
 
-def legendre_kernel(*refs, parts, pots, patches):
-    *table_refs, spectra_ref, out_ref = refs
+def legendre_kernel(*refs, levs, parts, pots, patches):
+    place_ref, *refs = refs
+    table_refs, spectra_refs, out_ref = refs[:levs], refs[levs:-1], refs[-1]
     wave_count, entries, _ = table_refs[0].shape
-    _, _, pair, level_count, _ = spectra_ref.shape
+    _, pair, level_count, _ = spectra_refs[0].shape
     half = level_count // pots
     width = pots * half
     groups = entries // (patches * SUB)
     lanes = groups * width
     rows = wave_count * pair
+    part, pot = place_ref[3], place_ref[4]
     rim = {}
     lane = lax.broadcasted_iota(jnp.int32, (1, lanes), 1)
     sub = lax.broadcasted_iota(jnp.int32, (rows, lanes), 0)
@@ -109,13 +111,15 @@
         table = table_refs[0][m]
         for other in table_refs[1:]:
             table = table + other[m]
-        columns = [
-            spectra_ref[e * pots + p, m, c, h * half : (h + 1) * half, :]
-            for e in range(parts)
-            for h in range(pots)
-            for c in range(pair)
-            for p in range(pots)
-        ]
+        columns = []
+        for e in range(parts):
+            own_ref, other_ref = spectra_refs[2 * e : 2 * e + 2]
+            at = (place_ref[0] if e == 0 else pot) * wave_count + m
+            for h in range(pots):
+                for c in range(pair):
+                    own = own_ref[at, c, h * half : (h + 1) * half, :]
+                    other = other_ref[at, c, h * half : (h + 1) * half, :]
+                    columns += [jnp.where(pot == 0, own, other), jnp.where(pot == 0, other, own)]
         product = dot_nt(table, jnp.concatenate(columns, axis=0))
         for e in range(parts):
             for h in range(pots):
@@ -130,8 +134,8 @@
                     )
                     row = m * pair + c
                     for q in range(patches):
-                        place = (e * patches + q) * pots + h
-                        out_ref[place, row * SUB : (row + 1) * SUB, :] = tile[
+                        spot = (lax.rem(part + parts - e, parts) * patches + q) * pots + h
+                        out_ref[spot, row * SUB : (row + 1) * SUB, :] = tile[
                             q * SUB : (q + 1) * SUB
                         ].astype(jnp.bfloat16)
                         after = (q + 1) % patches
@@ -141,28 +145,31 @@
                             tile[after * SUB : after * SUB + 1],
                             tile[before * SUB + SUB - 1 : before * SUB + SUB],
                         )
-                        rim[place] = (
-                            jnp.where(sub == row, edge, rim[place])
-                            if place in rim
+                        rim[e, q, h] = (
+                            jnp.where(sub == row, edge, rim[e, q, h])
+                            if (e, q, h) in rim
                             else jnp.broadcast_to(edge, (rows, lanes))
                         )
-    for place, value in rim.items():
-        out_ref[place, rows * SUB : rows * SUB + rows, :] = value.astype(jnp.bfloat16)
-
-
-def legendre_rows(tables, spectra, parts, pots, patches):
+    for (e, q, h), value in rim.items():
+        spot = (lax.rem(part + parts - e, parts) * patches + q) * pots + h
+        out_ref[spot, rows * SUB : rows * SUB + rows, :] = value.astype(jnp.bfloat16)
+
+
+def legendre_rows(place, tables, spectra, parts, pots, patches):
     wave_count, entries, _ = tables[0].shape
-    _, _, pair, level_count, _ = spectra.shape
+    _, pair, level_count, _ = spectra[0].shape
     lanes = entries // (patches * SUB) * level_count
     rows = wave_count * pair
     return pl.pallas_call(
-        functools.partial(legendre_kernel, parts=parts, pots=pots, patches=patches),
+        functools.partial(
+            legendre_kernel, levs=len(tables), parts=parts, pots=pots, patches=patches
+        ),
         out_shape=result((parts * patches * pots, rows * SUB + rows, lanes), jnp.bfloat16),
-        in_specs=[WHOLE] * (len(tables) + 1),
+        in_specs=[SCALARS] + [WHOLE] * (len(tables) + len(spectra)),
         out_specs=WHOLE,
         compiler_params=PARAMS,
         name="legendre_rows",
-    )(*in_vmem(*tables, spectra))
+    )(place, *in_vmem(*tables, *spectra))
 
 
 def lane_gather(values, index):
@@ -349,22 +356,27 @@
     share = lax.axis_index("ens") * pots + lax.axis_index("pot")
     own = lax.axis_index("wave")
 
-    place = jnp.stack([share, lax.axis_index("lev"), own]).astype(jnp.int32)
-    gathered = lax.all_to_all(
-        own_spectra.reshape(shares, wave_count, pair, level_count, degrees),
-        ("ens", "pot"),
-        split_axis=0,
-        concat_axis=0,
-        tiled=True,
-    )
+    part, pot = lax.axis_index("ens"), lax.axis_index("pot")
+    place = jnp.stack([share, lax.axis_index("lev"), own, part, pot]).astype(jnp.int32)
+
+    def over(axis, size, step):
+        return functools.partial(
+            lax.ppermute, axis_name=axis, perm=[(i, (i + step) % size) for i in range(size)]
+        )
+
+    held = [own_spectra]
+    for step in range(1, parts):
+        first = (part + step) % parts * pots * wave_count
+        block = lax.dynamic_slice_in_dim(own_spectra, first, pots * wave_count, axis=0)
+        held.append(over("ens", parts, step)(block))
     chosen = select_rows(place, row_map, legendre, wave_count)
-    tables = [chosen] + [
-        lax.ppermute(chosen, "lev", [(i, (i + s) % levs) for i in range(levs)])
-        for s in range(1, levs)
-    ]
+    tables = [chosen] + [over("lev", levs, step)(chosen) for step in range(1, levs)]
+    gathered = []
+    for x in held:
+        gathered += [x, over("pot", pots, 1)(x)]
     before = lax.ppermute(interp[0, -1], "wave", [(i, (i + 1) % waves) for i in range(waves)])
     after = lax.ppermute(interp[0, 0], "wave", [((i + 1) % waves, i) for i in range(waves)])
-    outgoing = legendre_rows(tables, gathered, parts, pots, row_map.shape[0])
+    outgoing = legendre_rows(place, tables, gathered, parts, pots, row_map.shape[0])
     incoming = lax.all_to_all(
         outgoing, ("ens", "wave", "pot"), split_axis=0, concat_axis=0, tiled=True
     )

time: 51.3 us -> 50.8 us (level)
  local copies, waits for them, and re-layouts: 0.62 us -> 2.75 us
  starting transfers between devices: 15.4 us -> 13.4 us
  waiting for transfers between devices: 13.5 us -> 11.9 us
  Pallas kernels: 14.4 us -> 15.4 us
    all_to_all x1 -> x0, waiting for transfers between devices: 5.99 us -> none  [body(): lax.all_to_all(own_spectra.reshape(shares, wave_count, pair, level_count,...]
    ppermute x1 -> x4, waiting for transfers between devices: 1.23 us -> 5.58 us  [the longest x1 2.86 us: body(): over('lev', levs, step)(chosen)]
    all_to_all x1 -> x0, starting transfers between devices: 3.52 us -> none  [body(): lax.all_to_all(own_spectra.reshape(shares, wave_count, pair, level_count,...]
    dynamic_slice x0 -> x1, local copies, waits for them, and re-layouts: none -> 2.04 us  [body(): lax.dynamic_slice_in_dim(own_spectra, first, pots * wave_count, axis=0)]
    ppermute x1 -> x4, starting transfers between devices: 3.04 us -> 4.57 us  [the longest x1 3 us: body(): held.append(over('ens', parts, step)(block))]
    pallas_call x1, Pallas kernels: 1.53 us -> 2.58 us  [legendre_rows(): pl.pallas_call(functools.partial(legendre_kernel, levs=len(tables), parts...]
  transfers between devices with their start and end apart: 5 -> 7, of which waited for: 3 -> 3; matrix products, arithmetic and copies ran while one was open for 15% -> 15% of each run, Pallas kernels for 3% -> 11%
where the time goes in v3:
time: 50.8 us; the launch traced here: 50.5 us
  Pallas kernels  15.4 us (30%)
  starting transfers between devices  13.4 us (26%)
  waiting for transfers between devices  11.9 us (23%)
  other arithmetic  7.03 us (14%)
  local copies, waits for them, and re-layouts  2.75 us (5%)
    pallas_call x1, Pallas kernels, patch_winds(): pl.pallas_call(patch_kernel, out_shape=jax.ShapeDtypeStruct((half, edges....  9.95 us
    all_to_all x1, waiting for transfers between devices, body(): lax.all_to_all(outgoing, ('ens', 'wave', 'pot'), split_axis=0, concat_axi...  6.29 us
    all_to_all x1, starting transfers between devices, body(): lax.all_to_all(outgoing, ('ens', 'wave', 'pot'), split_axis=0, concat_axi...  5 us
    convert_element_type x1, other arithmetic, fourier_segments(): return jnp.where(mode % 2 == 0, factor * jnp.cos(angle_values), -factor *...  4.22 us
    ppermute x1, starting transfers between devices, body(): held.append(over('ens', parts, step)(block))  3 us
    pallas_call x1, Pallas kernels, select_rows(): pl.pallas_call(select_kernel, out_shape=result((wave_count, patches * blo...  2.86 us
    ppermute x1, waiting for transfers between devices, body(): over('lev', levs, step)(chosen)  2.86 us
    ppermute x1, waiting for transfers between devices, body(): held.append(over('ens', parts, step)(block))  2.72 us
  transfers between devices with their start and end apart: 7, of which 3 were waited for; matrix products, arithmetic and copies ran while one was open for 15% of the time, Pallas kernels for 11%

profile of v3, /device:TPU:0, one launch (start us, length us, event | category | flops | bytes accessed | tf_op | source)
XLA Modules:
  0.0 50.5 jit_solution(9022550327619619250)
XLA Ops:
  0.0 2.0 %dynamic-slice_bitcast_fusion = bf16[8,2,32,512]{3,2,1,0:T(8,128)(2,1)} fusion(bf16[1,16,2,32,512]{4,3,2,1,0:T(8,128)(2,1)} %param.7, s32[]{:T(128)S(6)} %select_n.55), kind=kLoop, calls=%fused_computation.44 | loop fusion | bytes 1048580 | tf_op jit(solution)/shard_map/dynamic_slice | solution.py:370
  2.0 3.0 %collective-permute-start.2 = (bf16[8,2,32,512]{3,2,1,0:T(8,128)(2,1)}, bf16[8,2,32,512]{3,2,1,0:T(8,128)(2,1)}, u32[]{:S(2)}, u32[]{:S(2)}) collective-permute-start(bf16[8,2,32,512]{3,2,1,0:T(8,128)(2,1)} %dynamic-slice_bitcast_fusion), channel_id=1, source_target_pairs={{0,16},{16,0},{1,17},{17,1},{2,18},{18,2},{3,19},{19,3},{4,20},{20... | collective-permute-start | bytes 1572872 | tf_op jit(solution)/shard_map/ppermute | solution.py:371
  5.0 0.0 collective-permute-start.1
  5.0 0.1 stack.23.place_ref.refs_0_
  5.1 2.9 %select_rows.1.refs_1_ = bf16[4,128,512]{2,1,0:T(8,128)(2,1)S(1)} custom-call(s32[5]{0:T(128)S(1)} %stack.23.place_ref.refs_0_, s32[4,32]{1,0:T(4,128)} %map_ref.1, bf16[16,384,512]{2,1,0:T(8,128)(2,1)} %legendre_ref.1), custom_call_target="tpu_custom_call" | custom-call | tf_op jit(solution)/shard_map/select_rows/pallas_call | solution.py:81
  8.0 1.6 %collective-permute-start = (bf16[4,128,512]{2,1,0:T(8,128)(2,1)S(1)}, bf16[4,128,512]{2,1,0:T(8,128)(2,1)S(1)}, u32[]{:S(2)}, u32[]{:S(2)}) collective-permute-start(bf16[4,128,512]{2,1,0:T(8,128)(2,1)S(1)} %select_rows.1.refs_1_), channel_id=1, source_target_pairs={{0,2},{2,0},{1,3},{3,1},{4,6},{6,4},{5,7},{7,5},{8,10},{10,8},{9,1... | collective-permute-start | bytes 1572872 | tf_op jit(solution)/shard_map/ppermute | solution.py:373
  9.6 0.6 %slice_bitcast_fusion = (bf16[128,128]{1,0:T(8,128)(2,1)S(1)}, bf16[128,128]{1,0:T(8,128)(2,1)}) fusion(bf16[1,32,128,128]{3,2,1,0:T(8,128)(2,1)S(1)} %copy-done.1), kind=kLoop, calls=%fused_computation.45 | loop fusion | bytes 131072 | tf_op jit(solution)/shard_map/squeeze | solution.py:378
  10.2 1.6 %collective-permute-start.4 = (bf16[128,128]{1,0:T(8,128)(2,1)}, bf16[128,128]{1,0:T(8,128)(2,1)S(1)}, u32[]{:S(2)}, u32[]{:S(2)}) collective-permute-start(bf16[128,128]{1,0:T(8,128)(2,1)} %get-tuple-element.6), channel_id=1, source_target_pairs={{0,4},{4,8},{8,12},{12,0},{1,5},{5,9},{9,13},{13,1},{2,6},{6,10},{... | collective-permute-start | bytes 98312 | tf_op jit(solution)/shard_map/ppermute | solution.py:377
  11.7 2.3 %collective-permute-start.5 = (bf16[128,128]{1,0:T(8,128)(2,1)S(1)}, bf16[128,128]{1,0:T(8,128)(2,1)S(1)}, u32[]{:S(2)}, u32[]{:S(2)}) collective-permute-start(bf16[128,128]{1,0:T(8,128)(2,1)S(1)} %get-tuple-element.5), channel_id=1, source_target_pairs={{4,0},{8,4},{12,8},{0,12},{5,1},{9,5},{13,9},{1,13},{6,2},{10,6},{... | collective-permute-start | bytes 98312 | tf_op jit(solution)/shard_map/ppermute | solution.py:378
  14.0 0.5 %compare_and_fusion.2 = pred[128]{0:T(512)(128)(4,1)} fusion(), kind=kLoop, calls=%fused_computation.54 | loop fusion | flops 640 | bytes 128 | tf_op jit(solution)/shard_map/jit(floor_divide)/and | solution.py:340
  14.6 2.7 %collective-permute-done.2.refs_5_ = bf16[8,2,32,512]{3,2,1,0:T(8,128)(2,1)} collective-permute-done((bf16[8,2,32,512]{3,2,1,0:T(8,128)(2,1)}, bf16[8,2,32,512]{3,2,1,0:T(8,128)(2,1)}, u32[]{:S(2)}, u32[]{:S(2)}) %collective-permute-start.2) | collective-permute-done | bytes 524320 | tf_op jit(solution)/shard_map/ppermute | solution.py:371
  17.3 0.5 %iota_multiply_fusion = s32[12]{0:T(128)} fusion(), kind=kLoop, calls=%fused_computation.55 | loop fusion | flops 12 | bytes 48 | tf_op jit(solution)/shard_map/mul | solution.py:334
  17.8 0.6 %iota_and_fusion.1 = (s32[128]{0:T(128)}, s32[128]{0:T(128)}) fusion(), kind=kLoop, calls=%fused_computation.53 | loop fusion | flops 384 | bytes 1024 | tf_op jit(solution)/shard_map/jit(remainder)/rem | solution.py:345
  18.4 0.6 %broadcast_add_fusion.1 = (s32[128]{0:T(128)}, s32[128]{0:T(128)}) fusion(), kind=kLoop, calls=%fused_computation.57 | loop fusion | flops 512 | bytes 1024 | tf_op jit(solution)/shard_map/jit(floor_divide)/sub | solution.py:337
  19.0 0.6 %compare_and_fusion = (pred[128]{0:T(512)(128)(4,1)}, pred[128]{0:T(512)(128)(4,1)}) fusion(), kind=kLoop, calls=%fused_computation.47 | loop fusion | flops 1152 | bytes 256 | tf_op jit(solution)/shard_map/jit(floor_divide)/and | solution.py:337
  19.6 2.9 %collective-permute-done.refs_2_ = bf16[4,128,512]{2,1,0:T(8,128)(2,1)S(1)} collective-permute-done((bf16[4,128,512]{2,1,0:T(8,128)(2,1)S(1)}, bf16[4,128,512]{2,1,0:T(8,128)(2,1)S(1)}, u32[]{:S(2)}, u32[]{:S(2)}) %collective-permute-start) | collective-permute-done | bytes 524320 | tf_op jit(solution)/shard_map/ppermute | solution.py:373
  22.4 0.0 collective-permute-done.3.refs_6_
  22.4 0.0 collective-permute-done.1.refs_4_
  22.4 2.6 %legendre_rows.1 = bf16[16,72,128]{2,1,0:T(8,128)(2,1)} custom-call(s32[5]{0:T(128)S(1)} %stack.23.place_ref.refs_0_, bf16[4,128,512]{2,1,0:T(8,128)(2,1)S(1)} %select_rows.1.refs_1_, bf16[4,128,512]{2,1,0:T(8,128)(2,1)S(1)} %collective-permute-done.refs_2_, bf16[16,2,32,512]{3,2,1,0:T(8,128)(2,1)S(1)} %bitcast.16, ...), custom_call_target="tpu_custom_call" | custom-call | tf_op jit(solution)/shard_map/legendre_rows/pallas_call | solution.py:163
  25.0 5.0 %all-to-all-start = ((bf16[16,72,128]{2,1,0:T(8,128)(2,1)}), bf16[16,72,128]{2,1,0:T(8,128)(2,1)S(1)}, u32[]{:S(2)}, u32[]{:S(2)}) async-start(bf16[16,72,128]{2,1,0:T(8,128)(2,1)} %legendre_rows.1), calls=%async_computation | async-start | bytes 589824 | tf_op jit(solution)/shard_map/all_to_all | solution.py:380
  30.0 4.2 %fusion.1.fourier_ref = bf16[12,128,128]{2,1,0:T(8,128)(2,1)S(1)} fusion(s32[12]{0:T(128)} %iota_multiply_fusion, s32[128]{0:T(128)S(1)} %get-tuple-element.9, s32[128]{0:T(128)} %get-tuple-element.12, s32[128]{0:T(128)S(1)} %get-tuple-element.10, s32[128]{0:T(128)} %get-tuple-element.13, s32[128]{0:T(128)} %get-tuple-element.11, s32[128]{0:T(128)} %get-tuple-element.14, ...), kind=kLoop, calls=%fused_computation.23 | loop fusion | flops 15335424 | bytes 396720 | tf_op jit(solution)/shard_map/convert_element_type | solution.py:346
  34.2 0.0 collective-permute-done.4.before_ref
  34.3 6.3 %all-to-all-done.spectral_ref = bf16[16,72,128]{2,1,0:T(8,128)(2,1)S(1)} async-done(((bf16[16,72,128]{2,1,0:T(8,128)(2,1)}), bf16[16,72,128]{2,1,0:T(8,128)(2,1)S(1)}, u32[]{:S(2)}, u32[]{:S(2)}) %all-to-all-start) | async-done | bytes 294944 | tf_op jit(solution)/shard_map/all_to_all | solution.py:380
  40.6 9.9 %patch_winds.1 = bf16[16,12288]{1,0:T(8,128)(2,1)} custom-call(s32[5]{0:T(128)S(1)} %stack.23.place_ref.refs_0_, s32[4,32]{1,0:T(4,128)S(1)} %copy-done.4, bf16[16,72,128]{2,1,0:T(8,128)(2,1)S(1)} %all-to-all-done.spectral_ref, bf16[12,128,128]{2,1,0:T(8,128)(2,1)S(1)} %fusion.1.fourier_ref, bf16[32,128,128]{2,1,0:T(8,128)(2,1)S(1)} %bitcast.17, ...), custom_call_target="tpu_custom_call" | custom-call | tf_op jit(solution)/shard_map/patch_winds/pallas_call | solution.py:314
  (13 shorter events, 0.0 us)
Async XLA Ops:
  0.0 22.4 %copy-start = (bf16[1,16,2,32,512]{4,3,2,1,0:T(8,128)(2,1)S(1)}, bf16[1,16,2,32,512]{4,3,2,1,0:T(8,128)(2,1)}, u32[]{:S(2)}) copy-start(bf16[1,16,2,32,512]{4,3,2,1,0:T(8,128)(2,1)} %param.7) | copy-start | bytes 3145732
  0.0 9.6 %copy-start.1 = (bf16[1,32,128,128]{3,2,1,0:T(8,128)(2,1)S(1)}, bf16[1,32,128,128]{3,2,1,0:T(8,128)(2,1)}, u32[]{:S(2)}) copy-start(bf16[1,32,128,128]{3,2,1,0:T(8,128)(2,1)} %param.11) | copy-start | bytes 3145732
  2.0 15.2 %collective-permute-start.2 = (bf16[8,2,32,512]{3,2,1,0:T(8,128)(2,1)}, bf16[8,2,32,512]{3,2,1,0:T(8,128)(2,1)}, u32[]{:S(2)}, u32[]{:S(2)}) collective-permute-start(bf16[8,2,32,512]{3,2,1,0:T(8,128)(2,1)} %dynamic-slice_bitcast_fusion), channel_id=1, source_target_pairs={{0,16},{16,0},{1,17},{17,1},{2,18},{18,2},{3,19},{19,3},{4,20},{20... | collective-permute-start | bytes 1572872 | tf_op jit(solution)/shard_map/ppermute | solution.py:371
  5.0 17.4 %collective-permute-start.1 = (bf16[16,2,32,512]{3,2,1,0:T(8,128)(2,1)}, bf16[16,2,32,512]{3,2,1,0:T(8,128)(2,1)S(1)}, u32[]{:S(2)}, u32[]{:S(2)}) collective-permute-start(bf16[16,2,32,512]{3,2,1,0:T(8,128)(2,1)} %bitcast.15), channel_id=1, source_target_pairs={{0,1},{1,0},{2,3},{3,2},{4,5},{5,4},{6,7},{7,6},{8,9},{9,8},{10,11... | collective-permute-start | bytes 3145736 | tf_op jit(solution)/shard_map/ppermute | solution.py:376
  5.1 35.4 %copy-start.2 = (s32[1,4,12288]{2,1,0:T(4,128)S(1)}, s32[1,4,12288]{2,1,0:T(4,128)}, u32[]{:S(2)}) copy-start(s32[1,4,12288]{2,1,0:T(4,128)} %param.12) | copy-start | bytes 589828
  5.1 35.4 %copy-start.3 = (f32[1,2,12288]{2,1,0:T(2,128)S(1)}, f32[1,2,12288]{2,1,0:T(2,128)}, u32[]{:S(2)}) copy-start(f32[1,2,12288]{2,1,0:T(2,128)} %param.13) | copy-start | bytes 294916
  5.1 35.4 %copy-start.4 = (s32[4,32]{1,0:T(4,128)S(1)}, s32[4,32]{1,0:T(4,128)}, u32[]{:S(2)}) copy-start(s32[4,32]{1,0:T(4,128)} %seg_ref.1) | copy-start | bytes 1540
  8.0 14.4 %collective-permute-start = (bf16[4,128,512]{2,1,0:T(8,128)(2,1)S(1)}, bf16[4,128,512]{2,1,0:T(8,128)(2,1)S(1)}, u32[]{:S(2)}, u32[]{:S(2)}) collective-permute-start(bf16[4,128,512]{2,1,0:T(8,128)(2,1)S(1)} %select_rows.1.refs_1_), channel_id=1, source_target_pairs={{0,2},{2,0},{1,3},{3,1},{4,6},{6,4},{5,7},{7,5},{8,10},{10,8},{9,1... | collective-permute-start | bytes 1572872 | tf_op jit(solution)/shard_map/ppermute | solution.py:373
  10.2 24.1 %collective-permute-start.4 = (bf16[128,128]{1,0:T(8,128)(2,1)}, bf16[128,128]{1,0:T(8,128)(2,1)S(1)}, u32[]{:S(2)}, u32[]{:S(2)}) collective-permute-start(bf16[128,128]{1,0:T(8,128)(2,1)} %get-tuple-element.6), channel_id=1, source_target_pairs={{0,4},{4,8},{8,12},{12,0},{1,5},{5,9},{9,13},{13,1},{2,6},{6,10},{... | collective-permute-start | bytes 98312 | tf_op jit(solution)/shard_map/ppermute | solution.py:377
  11.7 22.5 %collective-permute-start.5 = (bf16[128,128]{1,0:T(8,128)(2,1)S(1)}, bf16[128,128]{1,0:T(8,128)(2,1)S(1)}, u32[]{:S(2)}, u32[]{:S(2)}) collective-permute-start(bf16[128,128]{1,0:T(8,128)(2,1)S(1)} %get-tuple-element.5), channel_id=1, source_target_pairs={{4,0},{8,4},{12,8},{0,12},{5,1},{9,5},{13,9},{1,13},{6,2},{10,6},{... | collective-permute-start | bytes 98312 | tf_op jit(solution)/shard_map/ppermute | solution.py:378
  17.3 5.1 %collective-permute-start.3 = (bf16[8,2,32,512]{3,2,1,0:T(8,128)(2,1)}, bf16[8,2,32,512]{3,2,1,0:T(8,128)(2,1)S(1)}, u32[]{:S(2)}, u32[]{:S(2)}) collective-permute-start(bf16[8,2,32,512]{3,2,1,0:T(8,128)(2,1)} %collective-permute-done.2.refs_5_), channel_id=1, source_target_pairs={{0,1},{1,0},{2,3},{3,2},{4,5},{5,4},{6,7},{7,6},{8,9},{9,8},{10,11... | collective-permute-start | bytes 1572872 | tf_op jit(solution)/shard_map/ppermute | solution.py:376
  25.0 15.5 %all-to-all-start = ((bf16[16,72,128]{2,1,0:T(8,128)(2,1)}), bf16[16,72,128]{2,1,0:T(8,128)(2,1)S(1)}, u32[]{:S(2)}, u32[]{:S(2)}) async-start(bf16[16,72,128]{2,1,0:T(8,128)(2,1)} %legendre_rows.1), calls=%async_computation | async-start | bytes 589824 | tf_op jit(solution)/shard_map/all_to_all | solution.py:380

commit v4 on v3

--- a/solution.py
+++ b/solution.py
@@ -40,21 +40,31 @@
     return pltpu.VMEM(shape, dtype) if fits(shape, dtype) else jax.ShapeDtypeStruct(shape, dtype)
 
 
-def select_kernel(place_ref, map_ref, legendre_ref, out_ref, rows_ref, held_ref, sems):
+def select_kernel(place_ref, map_ref, legendre_ref, spectra_ref, out_ref, *refs, parts, pots):
+    *piece_refs, rows_ref, held_ref, sems = refs
     patches, blocks = rows_ref.shape
     wave_count, rows_dev, _ = held_ref.shape
+    share, lev, part, pot = place_ref[0], place_ref[1], place_ref[3], place_ref[4]
+    rows_copy = pltpu.make_async_copy(map_ref, rows_ref, sems.at[wave_count])
+    rows_copy.start()
     copies = [
-        pltpu.make_async_copy(
-            legendre_ref.at[place_ref[0] * wave_count + m], held_ref.at[m], sems.at[m]
-        )
+        pltpu.make_async_copy(legendre_ref.at[share * wave_count + m], held_ref.at[m], sems.at[m])
         for m in range(wave_count)
     ]
-    for copy in copies:
+    pieces = []
+    for k, piece_ref in enumerate(piece_refs):
+        to = lax.rem(part + k // pots, parts) * pots + lax.rem(pot + k % pots, pots)
+        pieces.append(
+            pltpu.make_async_copy(
+                spectra_ref.at[pl.ds(to * wave_count, wave_count)],
+                piece_ref,
+                sems.at[wave_count + 1 + k],
+            )
+        )
+    for copy in copies + pieces:
         copy.start()
-    rows_copy = pltpu.make_async_copy(map_ref, rows_ref, sems.at[wave_count])
-    rows_copy.start()
     rows_copy.wait()
-    first = place_ref[1] * rows_dev
+    first = lev * rows_dev
     eye = lax.broadcasted_iota(jnp.int32, (blocks, blocks), 0) == lax.broadcasted_iota(
         jnp.int32, (blocks, blocks), 1
     )
@@ -73,24 +83,33 @@
         out_ref[m] = jnp.dot(onehot, held_ref[m], preferred_element_type=jnp.float32).astype(
             jnp.bfloat16
         )
-
-
-def select_rows(place, row_map, legendre, wave_count):
+    for piece in pieces:
+        piece.wait()
+
+
+def select_rows(place, row_map, legendre, spectra, parts, pots):
     _, rows_dev, degrees = legendre.shape
     patches, blocks = row_map.shape
+    waves, *rest = spectra.shape
+    shares = parts * pots
+    wave_count = waves // shares
     return pl.pallas_call(
-        select_kernel,
-        out_shape=result((wave_count, patches * blocks, degrees), jnp.bfloat16),
-        in_specs=[SCALARS, IN_HBM, IN_HBM],
-        out_specs=WHOLE,
+        functools.partial(select_kernel, parts=parts, pots=pots),
+        out_shape=[result((wave_count, patches * blocks, degrees), jnp.bfloat16)]
+        + [result((wave_count, *rest), jnp.bfloat16)] * shares,
+        in_specs=[SCALARS, IN_HBM, IN_HBM, IN_HBM],
+        out_specs=[WHOLE] * (1 + shares),
         scratch_shapes=[
             pltpu.VMEM((patches, blocks), jnp.int32),
             pltpu.VMEM((wave_count, rows_dev, degrees), jnp.bfloat16),
-            pltpu.SemaphoreType.DMA((wave_count + 1,)),
+            pltpu.SemaphoreType.DMA((wave_count + 1 + shares,)),
         ],
         compiler_params=PARAMS,
         name="select_rows",
-    )(place, *(pltpu.with_memory_space_constraint(x, pltpu.HBM) for x in (row_map, legendre)))
+    )(
+        place,
+        *(pltpu.with_memory_space_constraint(x, pltpu.HBM) for x in (row_map, legendre, spectra)),
+    )
 
 
 def legendre_kernel(*refs, levs, parts, pots, patches):
@@ -103,7 +122,7 @@
     groups = entries // (patches * SUB)
     lanes = groups * width
     rows = wave_count * pair
-    part, pot = place_ref[3], place_ref[4]
+    part = place_ref[3]
     rim = {}
     lane = lax.broadcasted_iota(jnp.int32, (1, lanes), 1)
     sub = lax.broadcasted_iota(jnp.int32, (rows, lanes), 0)
@@ -111,15 +130,13 @@
         table = table_refs[0][m]
         for other in table_refs[1:]:
             table = table + other[m]
-        columns = []
-        for e in range(parts):
-            own_ref, other_ref = spectra_refs[2 * e : 2 * e + 2]
-            at = (place_ref[0] if e == 0 else pot) * wave_count + m
-            for h in range(pots):
-                for c in range(pair):
-                    own = own_ref[at, c, h * half : (h + 1) * half, :]
-                    other = other_ref[at, c, h * half : (h + 1) * half, :]
-                    columns += [jnp.where(pot == 0, own, other), jnp.where(pot == 0, other, own)]
+        columns = [
+            spectra_refs[e * pots + p][m, c, h * half : (h + 1) * half, :]
+            for e in range(parts)
+            for h in range(pots)
+            for c in range(pair)
+            for p in range(pots)
+        ]
         product = dot_nt(table, jnp.concatenate(columns, axis=0))
         for e in range(parts):
             for h in range(pots):
@@ -249,11 +266,15 @@
     tall = cells_ref.shape[0] // pots
     windows = blocks * BLOCK // WINDOW
     own = place_ref[2]
+    pot_of_lane = lax.broadcasted_iota(jnp.int32, (chunk, lanes), 1) // half % pots
     for s in range(sources):
-        main_ref[s * rows * SUB : (s + 1) * rows * SUB, :] = spectral_ref[s, : rows * SUB].astype(
-            jnp.float32
-        )
-        rim_ref[s * rows : (s + 1) * rows, :] = spectral_ref[s, rows * SUB :].astype(jnp.float32)
+        lists = spectral_ref[s].astype(jnp.float32)
+        modes = lists
+        if s % pots:
+            ahead, behind = pltpu.roll(lists, half, 1), pltpu.roll(lists, lanes - half, 1)
+            modes = jnp.where(pot_of_lane == 0, behind, ahead)
+        main_ref[s * rows * SUB : (s + 1) * rows * SUB, :] = modes[: rows * SUB]
+        rim_ref[s * rows : (s + 1) * rows, :] = modes[rows * SUB :]
 
     def block_cells(modes, segment, weights, position):
         grid = jnp.dot(modes, fourier_ref[segment], preferred_element_type=jnp.float32)
@@ -359,21 +380,22 @@
     part, pot = lax.axis_index("ens"), lax.axis_index("pot")
     place = jnp.stack([share, lax.axis_index("lev"), own, part, pot]).astype(jnp.int32)
 
-    def over(axis, size, step):
-        return functools.partial(
-            lax.ppermute, axis_name=axis, perm=[(i, (i + step) % size) for i in range(size)]
-        )
-
-    held = [own_spectra]
-    for step in range(1, parts):
-        first = (part + step) % parts * pots * wave_count
-        block = lax.dynamic_slice_in_dim(own_spectra, first, pots * wave_count, axis=0)
-        held.append(over("ens", parts, step)(block))
-    chosen = select_rows(place, row_map, legendre, wave_count)
-    tables = [chosen] + [over("lev", levs, step)(chosen) for step in range(1, levs)]
-    gathered = []
-    for x in held:
-        gathered += [x, over("pot", pots, 1)(x)]
+    chosen, *pieces = select_rows(place, row_map, legendre, own_spectra, parts, pots)
+    tables = [chosen] + [
+        lax.ppermute(chosen, "lev", [(i, (i + step) % levs) for i in range(levs)])
+        for step in range(1, levs)
+    ]
+    gathered = pieces[:1]
+    for k in range(1, shares):
+        pairs = [
+            (
+                i * pots + j,
+                (i + k // pots) % parts * pots + (j + k % pots) % pots,
+            )
+            for i in range(parts)
+            for j in range(pots)
+        ]
+        gathered.append(lax.ppermute(pieces[k], ("ens", "pot"), pairs))
     before = lax.ppermute(interp[0, -1], "wave", [(i, (i + 1) % waves) for i in range(waves)])
     after = lax.ppermute(interp[0, 0], "wave", [((i + 1) % waves, i) for i in range(waves)])
     outgoing = legendre_rows(place, tables, gathered, parts, pots, row_map.shape[0])

time: 50.8 us -> 48.4 us (0.953)
  other arithmetic: 7.03 us -> 3.56 us
  waiting for transfers between devices: 11.9 us -> 15 us
  local copies, waits for them, and re-layouts: 2.75 us -> 0.1 us
  starting transfers between devices: 13.4 us -> 14.8 us
  Pallas kernels: 15.4 us -> 14.7 us
    ppermute x4, waiting for transfers between devices: 5.58 us -> 8.01 us  [the longest x3 8 us: body(): gathered.append(lax.ppermute(pieces[k], ('ens', 'pot'), pairs))]
    dynamic_slice x1 -> x0, local copies, waits for them, and re-layouts: 2.04 us -> none  [body(): lax.dynamic_slice_in_dim(own_spectra, first, pots * wave_count, axis=0)]
    all_to_all x1, starting transfers between devices: 5 us -> 5.94 us  [body(): lax.all_to_all(outgoing, ('ens', 'wave', 'pot'), split_axis=0, concat_axi...]
    all_to_all x1, waiting for transfers between devices: 6.29 us -> 6.98 us  [body(): lax.all_to_all(outgoing, ('ens', 'wave', 'pot'), split_axis=0, concat_axi...]
    convert_element_type x1, other arithmetic: 4.22 us -> 3.53 us  [fourier_segments(): return jnp.where(mode % 2 == 0, factor * jnp.cos(angle_values), -factor *...]
    squeeze x1, local copies, waits for them, and re-layouts: 0.61 us -> 0.01 us  [body(): interp[0, 0]]
    and x1, other arithmetic: 0.58 us -> 0.01 us  [fourier_segments(): source = mode // (2 * wave_count)]
    rem x1, other arithmetic: 0.58 us -> 0.01 us  [fourier_segments(): mode % 2 == 0]
  transfers between devices with their start and end apart: 7 -> 7, of which waited for: 3 -> 3; matrix products, arithmetic and copies ran while one was open for 15% -> 7% of each run, Pallas kernels for 11% -> 4%
where the time goes in v4:
time: 48.4 us; the launch traced here: 48.2 us
  waiting for transfers between devices  15 us (31%)
  starting transfers between devices  14.8 us (31%)
  Pallas kernels  14.7 us (30%)
  other arithmetic  3.56 us (7%)
    pallas_call x1, Pallas kernels, patch_winds(): pl.pallas_call(patch_kernel, out_shape=jax.ShapeDtypeStruct((half, edges....  10.1 us
    ppermute x3, waiting for transfers between devices, body(): gathered.append(lax.ppermute(pieces[k], ('ens', 'pot'), pairs))  8 us
    all_to_all x1, waiting for transfers between devices, body(): lax.all_to_all(outgoing, ('ens', 'wave', 'pot'), split_axis=0, concat_axi...  6.98 us
    all_to_all x1, starting transfers between devices, body(): lax.all_to_all(outgoing, ('ens', 'wave', 'pot'), split_axis=0, concat_axi...  5.94 us
    convert_element_type x1, other arithmetic, fourier_segments(): return jnp.where(mode % 2 == 0, factor * jnp.cos(angle_values), -factor *...  3.53 us
    ppermute x1, starting transfers between devices, body(): lax.ppermute(chosen, 'lev', [(i, (i + step) % levs) for i in range(levs)])  3.05 us
    pallas_call x1, Pallas kernels, select_rows(): pl.pallas_call(functools.partial(select_kernel, parts=parts, pots=pots),...  2.57 us
    ppermute x1, starting transfers between devices, body(): lax.ppermute(interp[0, 0], 'wave', [((i + 1) % waves, i) for i in range(w...  2.3 us
  transfers between devices with their start and end apart: 7, of which 3 were waited for; matrix products, arithmetic and copies ran while one was open for 7% of the time, Pallas kernels for 4%

profile of v4, /device:TPU:0, one launch (start us, length us, event | category | flops | bytes accessed | tf_op | source)
XLA Modules:
  0.0 48.2 jit_solution(14697681878893416162)
XLA Ops:
  0.0 0.0 copy-start
  0.0 0.1 stack.23.place_ref.refs_0_
  0.1 2.6 %select_rows.1 = (bf16[4,128,512]{2,1,0:T(8,128)(2,1)S(1)}, bf16[4,2,32,512]{3,2,1,0:T(8,128)(2,1)S(1)}, bf16[4,2,32,512]{3,2,1,0:T(8,128)(2,1)S(1)}, bf16[4,2,3...) custom-call(s32[5]{0:T(128)S(1)} %stack.23.place_ref.refs_0_, s32[4,32]{1,0:T(4,128)} %map_ref.1, ...), custom_call_target="tpu_custom_call" | custom-call | tf_op jit(solution)/shard_map/select_rows/pallas_call | solution.py:96
  2.7 3.1 %collective-permute-start = (bf16[4,128,512]{2,1,0:T(8,128)(2,1)S(1)}, bf16[4,128,512]{2,1,0:T(8,128)(2,1)S(1)}, u32[]{:S(2)}, u32[]{:S(2)}) collective-permute-start(bf16[4,128,512]{2,1,0:T(8,128)(2,1)S(1)} %get-tuple-element.10.refs_1_), channel_id=1, source_target_pairs={{0,2},{2,0},{1,3},{3,1},{4,6},{6,4},{5,7},{7,5},{8,10},{10,8},{9,1... | collective-permute-start | bytes 1572872 | tf_op jit(solution)/shard_map/ppermute | solution.py:385
  5.7 0.0 collective-permute-start.1
  5.7 1.5 %collective-permute-start.2 = (bf16[4,2,32,512]{3,2,1,0:T(8,128)(2,1)S(1)}, bf16[4,2,32,512]{3,2,1,0:T(8,128)(2,1)S(1)}, u32[]{:S(2)}, u32[]{:S(2)}) collective-permute-start(bf16[4,2,32,512]{3,2,1,0:T(8,128)(2,1)S(1)} %get-tuple-element.13), channel_id=1, source_target_pairs={{0,16},{1,17},{16,0},{17,1},{2,18},{3,19},{18,2},{19,3},{4,20},{5,... | collective-permute-start | bytes 786440 | tf_op jit(solution)/shard_map/ppermute | solution.py:398
  7.2 0.3 collective-permute-start.3
  7.6 0.0 copy-done
  7.6 1.6 %collective-permute-start.4 = (bf16[128,128]{1,0:T(8,128)(2,1)S(1)}, bf16[128,128]{1,0:T(8,128)(2,1)S(1)}, u32[]{:S(2)}, u32[]{:S(2)}) collective-permute-start(bf16[128,128]{1,0:T(8,128)(2,1)S(1)} %get-tuple-element.16), channel_id=1, source_target_pairs={{0,4},{4,8},{8,12},{12,0},{1,5},{5,9},{9,13},{13,1},{2,6},{6,10},{... | collective-permute-start | bytes 98312 | tf_op jit(solution)/shard_map/ppermute | solution.py:399
  9.3 0.0 collective-permute-done.1.refs_4_
  9.3 2.3 %collective-permute-start.5 = (bf16[128,128]{1,0:T(8,128)(2,1)S(1)}, bf16[128,128]{1,0:T(8,128)(2,1)S(1)}, u32[]{:S(2)}, u32[]{:S(2)}) collective-permute-start(bf16[128,128]{1,0:T(8,128)(2,1)S(1)} %get-tuple-element.15), channel_id=1, source_target_pairs={{4,0},{8,4},{12,8},{0,12},{5,1},{9,5},{13,9},{1,13},{6,2},{10,6},{... | collective-permute-start | bytes 98312 | tf_op jit(solution)/shard_map/ppermute | solution.py:400
  11.6 3.3 %collective-permute-done.2.refs_5_ = bf16[4,2,32,512]{3,2,1,0:T(8,128)(2,1)S(1)} collective-permute-done((bf16[4,2,32,512]{3,2,1,0:T(8,128)(2,1)S(1)}, bf16[4,2,32,512]{3,2,1,0:T(8,128)(2,1)S(1)}, u32[]{:S(2)}, u32[]{:S(2)}) %collective-permute-start.2) | collective-permute-done | bytes 262176 | tf_op jit(solution)/shard_map/ppermute | solution.py:398
  14.9 4.7 %collective-permute-done.3.refs_6_ = bf16[4,2,32,512]{3,2,1,0:T(8,128)(2,1)S(1)} collective-permute-done((bf16[4,2,32,512]{3,2,1,0:T(8,128)(2,1)S(1)}, bf16[4,2,32,512]{3,2,1,0:T(8,128)(2,1)S(1)}, u32[]{:S(2)}, u32[]{:S(2)}) %collective-permute-start.3) | collective-permute-done | bytes 262176 | tf_op jit(solution)/shard_map/ppermute | solution.py:398
  19.6 0.0 collective-permute-done.refs_2_
  19.6 2.1 %legendre_rows.1 = bf16[16,72,128]{2,1,0:T(8,128)(2,1)} custom-call(s32[5]{0:T(128)S(1)} %stack.23.place_ref.refs_0_, bf16[4,128,512]{2,1,0:T(8,128)(2,1)S(1)} %get-tuple-element.10.refs_1_, bf16[4,128,512]{2,1,0:T(8,128)(2,1)S(1)} %collective-permute-done.refs_2_, bf16[4,2,32,512]{3,2,1,0:T(8,128)(2,1)S(1)} %get-tuple-element.11.refs_3_, ...), custom_call_target="tpu_custom_call" | custom-call | tf_op jit(solution)/shard_map/legendre_rows/pallas_call | solution.py:180
  21.7 5.9 %all-to-all-start = ((bf16[16,72,128]{2,1,0:T(8,128)(2,1)}), bf16[16,72,128]{2,1,0:T(8,128)(2,1)S(1)}, u32[]{:S(2)}, u32[]{:S(2)}) async-start(bf16[16,72,128]{2,1,0:T(8,128)(2,1)} %legendre_rows.1), calls=%async_computation | async-start | bytes 589824 | tf_op jit(solution)/shard_map/all_to_all | solution.py:402
  27.6 3.5 %fusion.1.fourier_ref = bf16[12,128,128]{2,1,0:T(8,128)(2,1)S(1)} fusion(s32[12]{0:T(128)S(1)} %iota_multiply_fusion, s32[128]{0:T(128)S(1)} %get-tuple-element.19, s32[128]{0:T(128)S(1)} %get-tuple-element.22, s32[128]{0:T(128)S(1)} %get-tuple-element.20, s32[128]{0:T(128)S(1)} %get-tuple-element.23, s32[128]{0:T(128)S(1)} %get-tuple-element.21, ...), kind=kLoop, calls=%fused_computation.23 | loop fusion | flops 15335424 | bytes 396720 | tf_op jit(solution)/shard_map/convert_element_type | solution.py:367
  31.2 0.0 collective-permute-done.4.before_ref
  31.2 0.0 collective-permute-done.5.after_ref
  31.2 7.0 %all-to-all-done.spectral_ref = bf16[16,72,128]{2,1,0:T(8,128)(2,1)S(1)} async-done(((bf16[16,72,128]{2,1,0:T(8,128)(2,1)}), bf16[16,72,128]{2,1,0:T(8,128)(2,1)S(1)}, u32[]{:S(2)}, u32[]{:S(2)}) %all-to-all-start) | async-done | bytes 294944 | tf_op jit(solution)/shard_map/all_to_all | solution.py:402
  38.2 0.0 copy-done.2
  38.2 0.0 copy-done.1
  38.2 0.0 copy-done.3
  38.2 10.1 %patch_winds.1 = bf16[16,12288]{1,0:T(8,128)(2,1)} custom-call(s32[5]{0:T(128)S(1)} %stack.23.place_ref.refs_0_, s32[4,32]{1,0:T(4,128)S(1)} %copy-done.3, bf16[16,72,128]{2,1,0:T(8,128)(2,1)S(1)} %all-to-all-done.spectral_ref, bf16[12,128,128]{2,1,0:T(8,128)(2,1)S(1)} %fusion.1.fourier_ref, bf16[32,128,128]{2,1,0:T(8,128)(2,1)S(1)} %bitcast.13, ...), custom_call_target="tpu_custom_call" | custom-call | tf_op jit(solution)/shard_map/patch_winds/pallas_call | solution.py:335
  (10 shorter events, 0.0 us)
Async XLA Ops:
  0.0 7.6 %copy-start = (bf16[1,32,128,128]{3,2,1,0:T(8,128)(2,1)S(1)}, bf16[1,32,128,128]{3,2,1,0:T(8,128)(2,1)}, u32[]{:S(2)}) copy-start(bf16[1,32,128,128]{3,2,1,0:T(8,128)(2,1)} %param.11) | copy-start | bytes 3145732
  0.0 38.2 %copy-start.2 = (f32[1,2,12288]{2,1,0:T(2,128)S(1)}, f32[1,2,12288]{2,1,0:T(2,128)}, u32[]{:S(2)}) copy-start(f32[1,2,12288]{2,1,0:T(2,128)} %param.13) | copy-start | bytes 294916
  0.0 38.2 %copy-start.1 = (s32[1,4,12288]{2,1,0:T(4,128)S(1)}, s32[1,4,12288]{2,1,0:T(4,128)}, u32[]{:S(2)}) copy-start(s32[1,4,12288]{2,1,0:T(4,128)} %param.12) | copy-start | bytes 589828
  0.0 38.2 %copy-start.3 = (s32[4,32]{1,0:T(4,128)S(1)}, s32[4,32]{1,0:T(4,128)}, u32[]{:S(2)}) copy-start(s32[4,32]{1,0:T(4,128)} %seg_ref.1) | copy-start | bytes 1540
  2.7 16.9 %collective-permute-start = (bf16[4,128,512]{2,1,0:T(8,128)(2,1)S(1)}, bf16[4,128,512]{2,1,0:T(8,128)(2,1)S(1)}, u32[]{:S(2)}, u32[]{:S(2)}) collective-permute-start(bf16[4,128,512]{2,1,0:T(8,128)(2,1)S(1)} %get-tuple-element.10.refs_1_), channel_id=1, source_target_pairs={{0,2},{2,0},{1,3},{3,1},{4,6},{6,4},{5,7},{7,5},{8,10},{10,8},{9,1... | collective-permute-start | bytes 1572872 | tf_op jit(solution)/shard_map/ppermute | solution.py:385
  5.7 3.6 %collective-permute-start.1 = (bf16[4,2,32,512]{3,2,1,0:T(8,128)(2,1)S(1)}, bf16[4,2,32,512]{3,2,1,0:T(8,128)(2,1)S(1)}, u32[]{:S(2)}, u32[]{:S(2)}) collective-permute-start(bf16[4,2,32,512]{3,2,1,0:T(8,128)(2,1)S(1)} %get-tuple-element.12), channel_id=1, source_target_pairs={{0,1},{1,0},{16,17},{17,16},{2,3},{3,2},{18,19},{19,18},{4,5},{5,4... | collective-permute-start | bytes 786440 | tf_op jit(solution)/shard_map/ppermute | solution.py:398
  5.7 9.2 %collective-permute-start.2 = (bf16[4,2,32,512]{3,2,1,0:T(8,128)(2,1)S(1)}, bf16[4,2,32,512]{3,2,1,0:T(8,128)(2,1)S(1)}, u32[]{:S(2)}, u32[]{:S(2)}) collective-permute-start(bf16[4,2,32,512]{3,2,1,0:T(8,128)(2,1)S(1)} %get-tuple-element.13), channel_id=1, source_target_pairs={{0,16},{1,17},{16,0},{17,1},{2,18},{3,19},{18,2},{19,3},{4,20},{5,... | collective-permute-start | bytes 786440 | tf_op jit(solution)/shard_map/ppermute | solution.py:398
  7.2 12.4 %collective-permute-start.3 = (bf16[4,2,32,512]{3,2,1,0:T(8,128)(2,1)S(1)}, bf16[4,2,32,512]{3,2,1,0:T(8,128)(2,1)S(1)}, u32[]{:S(2)}, u32[]{:S(2)}) collective-permute-start(bf16[4,2,32,512]{3,2,1,0:T(8,128)(2,1)S(1)} %get-tuple-element.14), channel_id=1, source_target_pairs={{0,17},{1,16},{16,1},{17,0},{2,19},{3,18},{18,3},{19,2},{4,21},{5,... | collective-permute-start | bytes 786440 | tf_op jit(solution)/shard_map/ppermute | solution.py:398
  7.6 23.6 %collective-permute-start.4 = (bf16[128,128]{1,0:T(8,128)(2,1)S(1)}, bf16[128,128]{1,0:T(8,128)(2,1)S(1)}, u32[]{:S(2)}, u32[]{:S(2)}) collective-permute-start(bf16[128,128]{1,0:T(8,128)(2,1)S(1)} %get-tuple-element.16), channel_id=1, source_target_pairs={{0,4},{4,8},{8,12},{12,0},{1,5},{5,9},{9,13},{13,1},{2,6},{6,10},{... | collective-permute-start | bytes 98312 | tf_op jit(solution)/shard_map/ppermute | solution.py:399
  9.3 21.9 %collective-permute-start.5 = (bf16[128,128]{1,0:T(8,128)(2,1)S(1)}, bf16[128,128]{1,0:T(8,128)(2,1)S(1)}, u32[]{:S(2)}, u32[]{:S(2)}) collective-permute-start(bf16[128,128]{1,0:T(8,128)(2,1)S(1)} %get-tuple-element.15), channel_id=1, source_target_pairs={{4,0},{8,4},{12,8},{0,12},{5,1},{9,5},{13,9},{1,13},{6,2},{10,6},{... | collective-permute-start | bytes 98312 | tf_op jit(solution)/shard_map/ppermute | solution.py:400
  21.7 16.5 %all-to-all-start = ((bf16[16,72,128]{2,1,0:T(8,128)(2,1)}), bf16[16,72,128]{2,1,0:T(8,128)(2,1)S(1)}, u32[]{:S(2)}, u32[]{:S(2)}) async-start(bf16[16,72,128]{2,1,0:T(8,128)(2,1)} %legendre_rows.1), calls=%async_computation | async-start | bytes 589824 | tf_op jit(solution)/shard_map/all_to_all | solution.py:402

commit v5 on v4

--- a/solution.py
+++ b/solution.py
@@ -15,7 +15,7 @@
 LANE = 128
 WINDOW = 2 * LANE
 WHOLE = pl.BlockSpec(memory_space=pltpu.VMEM)
-VMEM_ARRAY = 1 << 20
+VMEM_ARRAY = 2 << 20
 PARAMS = pltpu.CompilerParams(vmem_limit_bytes=32 << 20)
 IN_HBM = pl.BlockSpec(memory_space=pltpu.HBM)
 SCALARS = pl.BlockSpec(memory_space=pltpu.SMEM)
@@ -112,9 +112,11 @@
     )
 
 
-def legendre_kernel(*refs, levs, parts, pots, patches):
-    place_ref, *refs = refs
-    table_refs, spectra_refs, out_ref = refs[:levs], refs[levs:-1], refs[-1]
+def legendre_kernel(place_ref, *refs, order, parts, pots, patches):
+    *given, out_ref, held_ref = refs
+    shares = parts * pots
+    spectra_refs = [given[order.index(k)] for k in range(shares)]
+    table_refs = [given[i] for i, k in enumerate(order) if k >= shares]
     wave_count, entries, _ = table_refs[0].shape
     _, pair, level_count, _ = spectra_refs[0].shape
     half = level_count // pots
@@ -151,8 +153,7 @@
                     )
                     row = m * pair + c
                     for q in range(patches):
-                        spot = (lax.rem(part + parts - e, parts) * patches + q) * pots + h
-                        out_ref[spot, row * SUB : (row + 1) * SUB, :] = tile[
+                        held_ref[e, q * pots + h, row * SUB : (row + 1) * SUB, :] = tile[
                             q * SUB : (q + 1) * SUB
                         ].astype(jnp.bfloat16)
                         after = (q + 1) % patches
@@ -168,25 +169,34 @@
                             else jnp.broadcast_to(edge, (rows, lanes))
                         )
     for (e, q, h), value in rim.items():
-        spot = (lax.rem(part + parts - e, parts) * patches + q) * pots + h
-        out_ref[spot, rows * SUB : rows * SUB + rows, :] = value.astype(jnp.bfloat16)
+        held_ref[e, q * pots + h, rows * SUB : rows * SUB + rows, :] = value.astype(jnp.bfloat16)
+    for e in range(parts):
+        out_ref[lax.rem(part + parts - e, parts)] = held_ref[e]
 
 
 def legendre_rows(place, tables, spectra, parts, pots, patches):
+    shares = parts * pots
+    across = range(pots, shares, pots)
+    order = [*across, *range(shares, shares + len(tables))]
+    order += [k for k in range(shares - 1, -1, -1) if k not in across]
+    given = [tables[k - shares] if k >= shares else spectra[k] for k in order]
     wave_count, entries, _ = tables[0].shape
     _, pair, level_count, _ = spectra[0].shape
     lanes = entries // (patches * SUB) * level_count
     rows = wave_count * pair
     return pl.pallas_call(
         functools.partial(
-            legendre_kernel, levs=len(tables), parts=parts, pots=pots, patches=patches
+            legendre_kernel, order=order, parts=parts, pots=pots, patches=patches
         ),
-        out_shape=result((parts * patches * pots, rows * SUB + rows, lanes), jnp.bfloat16),
-        in_specs=[SCALARS] + [WHOLE] * (len(tables) + len(spectra)),
+        out_shape=result((parts, patches * pots, rows * SUB + rows, lanes), jnp.bfloat16),
+        in_specs=[SCALARS] + [WHOLE] * len(given),
         out_specs=WHOLE,
+        scratch_shapes=[
+            pltpu.VMEM((parts, patches * pots, rows * SUB + rows, lanes), jnp.bfloat16)
+        ],
         compiler_params=PARAMS,
         name="legendre_rows",
-    )(place, *in_vmem(*tables, *spectra))
+    )(place, *in_vmem(*given)).reshape(parts * patches * pots, rows * SUB + rows, lanes)
 
 
 def lane_gather(values, index):
@@ -252,20 +262,46 @@
     return [at[1] - at[0], at[3] - at[2]]
 
 
+def weights_kernel(place_ref, seg_ref, fourier_ref, interp_ref, before_ref, after_ref, out_ref):
+    patches, blocks = seg_ref.shape
+    own = place_ref[2]
+
+    def block_weights(segment, weights):
+        return dot_nt(fourier_ref[segment], weights).astype(jnp.bfloat16)
+
+    before = lax.rem(own + patches - 1, patches)
+    after = lax.rem(own + 1, patches)
+    out_ref[0] = block_weights(seg_ref[before, blocks - 1], before_ref[...])
+    for b in range(blocks):
+        out_ref[b + 1] = block_weights(seg_ref[own, b], interp_ref[b])
+    out_ref[blocks + 1] = block_weights(seg_ref[after, 0], after_ref[...])
+
+
+def block_weights(place, seg_map, fourier, interp, before, after):
+    blocks = interp.shape[0]
+    return pl.pallas_call(
+        weights_kernel,
+        out_shape=result((blocks + 2, fourier.shape[1], BLOCK), jnp.bfloat16),
+        in_specs=[SCALARS, SCALARS] + [WHOLE] * 4,
+        out_specs=WHOLE,
+        compiler_params=PARAMS,
+        name="block_weights",
+    )(place, seg_map, *in_vmem(fourier, interp, before, after))
+
+
 def patch_kernel(
-    place_ref, seg_ref, spectral_ref, fourier_ref, interp_ref, before_ref, after_ref, edges_ref,
-    lengths_ref, out_ref, main_ref, rim_ref, cells_ref, tables_ref,
+    spectral_ref, weights_ref, edges_ref, lengths_ref, out_ref,
+    main_ref, rim_ref, cells_ref, tables_ref,
 ):
     sources, chunk, lanes = spectral_ref.shape
     rows = chunk // (SUB + 1)
-    patches, blocks = seg_ref.shape
+    blocks = weights_ref.shape[0] - 2
     groups = blocks // SUB
     width = lanes // groups
     half = out_ref.shape[0]
     pots, _, _ = tables_ref.shape
     tall = cells_ref.shape[0] // pots
     windows = blocks * BLOCK // WINDOW
-    own = place_ref[2]
     pot_of_lane = lax.broadcasted_iota(jnp.int32, (chunk, lanes), 1) // half % pots
     for s in range(sources):
         lists = spectral_ref[s].astype(jnp.float32)
@@ -276,9 +312,11 @@
         main_ref[s * rows * SUB : (s + 1) * rows * SUB, :] = modes[: rows * SUB]
         rim_ref[s * rows : (s + 1) * rows, :] = modes[rows * SUB :]
 
-    def block_cells(modes, segment, weights, position):
-        grid = jnp.dot(modes, fourier_ref[segment], preferred_element_type=jnp.float32)
-        cells = dot_nt(grid.astype(jnp.bfloat16), weights).astype(jnp.bfloat16)
+    def block_cells(modes, block):
+        cells = jnp.dot(
+            modes, weights_ref[block], preferred_element_type=jnp.float32
+        ).astype(jnp.bfloat16)
+        position = block * BLOCK
         row = position // WINDOW * tall
         column = position % WINDOW
         for p in range(pots):
@@ -289,15 +327,10 @@
     for s in range(SUB):
         modes = main_ref[pl.ds(s, sources * rows, stride=SUB), :].T.astype(jnp.bfloat16)
         for g in range(groups):
-            b = g * SUB + s
-            block_cells(
-                modes[g * width : (g + 1) * width], seg_ref[own, b], interp_ref[b], HALO + b * BLOCK
-            )
+            block_cells(modes[g * width : (g + 1) * width], g * SUB + s + 1)
     modes = rim_ref[...].T.astype(jnp.bfloat16)
-    before = lax.rem(own + patches - 1, patches)
-    after = lax.rem(own + 1, patches)
-    block_cells(modes[(groups - 1) * width :], seg_ref[before, blocks - 1], before_ref[...], 0)
-    block_cells(modes[:width], seg_ref[after, 0], after_ref[...], HALO + blocks * BLOCK)
+    block_cells(modes[(groups - 1) * width :], 0)
+    block_cells(modes[:width], blocks + 1)
 
     def finish(sums, base, count):
         across = lengths_ref[pl.ds(0, 1), pl.ds(base, count)]
@@ -324,10 +357,10 @@
     lax.fori_loop(0, spans // repeat, edge_chunk, 0)
 
 
-def patch_winds(place, seg_map, spectral, fourier, interp, before, after, edges, lengths, pots):
+def patch_winds(spectral, weights, edges, lengths, pots):
     sources, chunk, lanes = spectral.shape
     rows = chunk // (SUB + 1)
-    _, blocks = seg_map.shape
+    blocks = weights.shape[0] - 2
     groups = blocks // SUB
     half = lanes // groups // pots
     tall = -(-half // (2 * SUB)) * 2 * SUB
@@ -335,7 +368,7 @@
     return pl.pallas_call(
         patch_kernel,
         out_shape=jax.ShapeDtypeStruct((half, edges.shape[1]), jnp.bfloat16),
-        in_specs=[SCALARS, SCALARS] + [WHOLE] * 7,
+        in_specs=[WHOLE] * 4,
         out_specs=WHOLE,
         scratch_shapes=[
             pltpu.VMEM((sources * rows * SUB, lanes), jnp.float32),
@@ -345,7 +378,7 @@
         ],
         compiler_params=PARAMS,
         name="patch_winds",
-    )(place, seg_map, *in_vmem(spectral, fourier, interp, before, after, edges, lengths))
+    )(*in_vmem(spectral, weights, edges, lengths))
 
 
 def fourier_segments(parts, waves, pots, wave_count, own_waves):
@@ -381,21 +414,21 @@
     place = jnp.stack([share, lax.axis_index("lev"), own, part, pot]).astype(jnp.int32)
 
     chosen, *pieces = select_rows(place, row_map, legendre, own_spectra, parts, pots)
+    def deal(k):
+        pairs = [
+            (i * pots + j, (i + k // pots) % parts * pots + (j + k % pots) % pots)
+            for i in range(parts)
+            for j in range(pots)
+        ]
+        return lax.ppermute(pieces[k], ("ens", "pot"), pairs)
+
+    dealt = {k: deal(k) for k in range(pots, shares, pots)}
     tables = [chosen] + [
         lax.ppermute(chosen, "lev", [(i, (i + step) % levs) for i in range(levs)])
         for step in range(1, levs)
     ]
-    gathered = pieces[:1]
-    for k in range(1, shares):
-        pairs = [
-            (
-                i * pots + j,
-                (i + k // pots) % parts * pots + (j + k % pots) % pots,
-            )
-            for i in range(parts)
-            for j in range(pots)
-        ]
-        gathered.append(lax.ppermute(pieces[k], ("ens", "pot"), pairs))
+    dealt.update({k: deal(k) for k in range(shares - 1, 0, -1) if k % pots})
+    gathered = [pieces[0]] + [dealt[k] for k in range(1, shares)]
     before = lax.ppermute(interp[0, -1], "wave", [(i, (i + 1) % waves) for i in range(waves)])
     after = lax.ppermute(interp[0, 0], "wave", [((i + 1) % waves, i) for i in range(waves)])
     outgoing = legendre_rows(place, tables, gathered, parts, pots, row_map.shape[0])
@@ -403,9 +436,8 @@
         outgoing, ("ens", "wave", "pot"), split_axis=0, concat_axis=0, tiled=True
     )
     fourier = fourier_segments(parts, waves, pots, wave_count, own_waves)
-    return patch_winds(
-        place, seg_map, incoming, fourier, interp[0], before, after, edges[0], inv_len[0], pots
-    )
+    weights = block_weights(place, seg_map, fourier, interp[0], before, after)
+    return patch_winds(incoming, weights, edges[0], inv_len[0], pots)
 
 
 def solution(mesh):

time: 48.4 us -> 44.9 us (0.928)
  waiting for transfers between devices: 15 us -> 10.9 us
  starting transfers between devices: 14.8 us -> 16.4 us
  Pallas kernels: 14.7 us -> 13.7 us
    ppermute x3, waiting for transfers between devices: 8 us -> 5.34 us  [deal(): return lax.ppermute(pieces[k], ('ens', 'pot'), pairs)]
    pallas_call x1, Pallas kernels: 10.1 us -> 7.51 us  [patch_winds(): pl.pallas_call(patch_kernel, out_shape=jax.ShapeDtypeStruct((half, edges....]
    pallas_call x1 -> x2, Pallas kernels: 2.07 us -> 3.63 us  [the longest x1 2.16 us: legendre_rows(): pl.pallas_call(functools.partial(legendre_kernel, order=order, parts=part...]
    all_to_all x1, waiting for transfers between devices: 6.98 us -> 5.5 us  [body(): lax.all_to_all(outgoing, ('ens', 'wave', 'pot'), split_axis=0, concat_axi...]
    ppermute x1, starting transfers between devices: 2.3 us -> 3.59 us  [body(): lax.ppermute(interp[0, 0], 'wave', [((i + 1) % waves, i) for i in range(w...]
  transfers between devices with their start and end apart: 7 -> 7, of which waited for: 3 -> 2; matrix products, arithmetic and copies ran while one was open for 7% -> 8% of each run, Pallas kernels for 4% -> 8%
where the time goes in v5:
time: 44.9 us; the launch traced here: 44.7 us
  starting transfers between devices  16.4 us (37%)
  Pallas kernels  13.7 us (31%)
  waiting for transfers between devices  10.9 us (24%)
  other arithmetic  3.56 us (8%)
    pallas_call x1, Pallas kernels, patch_winds(): pl.pallas_call(patch_kernel, out_shape=jax.ShapeDtypeStruct((half, edges....  7.51 us
    all_to_all x1, starting transfers between devices, body(): lax.all_to_all(outgoing, ('ens', 'wave', 'pot'), split_axis=0, concat_axi...  5.96 us
    all_to_all x1, waiting for transfers between devices, body(): lax.all_to_all(outgoing, ('ens', 'wave', 'pot'), split_axis=0, concat_axi...  5.5 us
    ppermute x3, waiting for transfers between devices, deal(): return lax.ppermute(pieces[k], ('ens', 'pot'), pairs)  5.34 us
    ppermute x1, starting transfers between devices, body(): lax.ppermute(interp[0, 0], 'wave', [((i + 1) % waves, i) for i in range(w...  3.59 us
    convert_element_type x1, other arithmetic, fourier_segments(): return jnp.where(mode % 2 == 0, factor * jnp.cos(angle_values), -factor *...  3.53 us
    ppermute x1, starting transfers between devices, body(): lax.ppermute(chosen, 'lev', [(i, (i + step) % levs) for i in range(levs)])  3.05 us
    pallas_call x1, Pallas kernels, select_rows(): pl.pallas_call(functools.partial(select_kernel, parts=parts, pots=pots),...  2.57 us
  transfers between devices with their start and end apart: 7, of which 2 were waited for; matrix products, arithmetic and copies ran while one was open for 8% of the time, Pallas kernels for 8%

profile of v5, /device:TPU:0, one launch (start us, length us, event | category | flops | bytes accessed | tf_op | source)
XLA Modules:
  0.0 44.7 jit_solution(12281231010568242034)
XLA Ops:
  0.0 0.1 stack.23.place_ref
  0.1 2.6 %select_rows.1 = (bf16[4,128,512]{2,1,0:T(8,128)(2,1)S(1)}, bf16[4,2,32,512]{3,2,1,0:T(8,128)(2,1)S(1)}, bf16[4,2,32,512]{3,2,1,0:T(8,128)(2,1)S(1)}, bf16[4,2,3...) custom-call(s32[5]{0:T(128)S(1)} %stack.23.place_ref, s32[4,32]{1,0:T(4,128)} %map_ref.1, ...), custom_call_target="tpu_custom_call" | custom-call | tf_op jit(solution)/shard_map/select_rows/pallas_call | solution.py:96
  2.7 3.0 %collective-permute-start.1 = (bf16[4,128,512]{2,1,0:T(8,128)(2,1)S(1)}, bf16[4,128,512]{2,1,0:T(8,128)(2,1)S(1)}, u32[]{:S(2)}, u32[]{:S(2)}) collective-permute-start(bf16[4,128,512]{2,1,0:T(8,128)(2,1)S(1)} %get-tuple-element.11.refs_1_), channel_id=1, source_target_pairs={{0,2},{2,0},{1,3},{3,1},{4,6},{6,4},{5,7},{7,5},{8,10},{10,8},{9,1... | collective-permute-start | bytes 1572872 | tf_op jit(solution)/shard_map/ppermute | solution.py:427
  5.7 1.5 %collective-permute-start = (bf16[4,2,32,512]{3,2,1,0:T(8,128)(2,1)S(1)}, bf16[4,2,32,512]{3,2,1,0:T(8,128)(2,1)S(1)}, u32[]{:S(2)}, u32[]{:S(2)}) collective-permute-start(bf16[4,2,32,512]{3,2,1,0:T(8,128)(2,1)S(1)} %get-tuple-element.10), channel_id=1, source_target_pairs={{0,16},{1,17},{16,0},{17,1},{2,18},{3,19},{18,2},{19,3},{4,20},{5,... | collective-permute-start | bytes 786440 | tf_op jit(solution)/shard_map/ppermute | solution.py:423
  7.2 0.0 collective-permute-start.2
  7.2 0.6 %collective-permute-start.3 = (bf16[4,2,32,512]{3,2,1,0:T(8,128)(2,1)S(1)}, bf16[4,2,32,512]{3,2,1,0:T(8,128)(2,1)S(1)}, u32[]{:S(2)}, u32[]{:S(2)}) collective-permute-start(bf16[4,2,32,512]{3,2,1,0:T(8,128)(2,1)S(1)} %get-tuple-element.13), channel_id=1, source_target_pairs={{0,1},{1,0},{16,17},{17,16},{2,3},{3,2},{18,19},{19,18},{4,5},{5,4... | collective-permute-start | bytes 786440 | tf_op jit(solution)/shard_map/ppermute | solution.py:423
  7.9 0.0 copy-done
  7.9 1.6 %collective-permute-start.4 = (bf16[128,128]{1,0:T(8,128)(2,1)S(1)}, bf16[128,128]{1,0:T(8,128)(2,1)S(1)}, u32[]{:S(2)}, u32[]{:S(2)}) collective-permute-start(bf16[128,128]{1,0:T(8,128)(2,1)S(1)} %get-tuple-element.16), channel_id=1, source_target_pairs={{0,4},{4,8},{8,12},{12,0},{1,5},{5,9},{9,13},{13,1},{2,6},{6,10},{... | collective-permute-start | bytes 98312 | tf_op jit(solution)/shard_map/ppermute | solution.py:432
  9.6 5.3 %collective-permute-done.refs_0_ = bf16[4,2,32,512]{3,2,1,0:T(8,128)(2,1)S(1)} collective-permute-done((bf16[4,2,32,512]{3,2,1,0:T(8,128)(2,1)S(1)}, bf16[4,2,32,512]{3,2,1,0:T(8,128)(2,1)S(1)}, u32[]{:S(2)}, u32[]{:S(2)}) %collective-permute-start) | collective-permute-done | bytes 262176 | tf_op jit(solution)/shard_map/ppermute | solution.py:423
  14.9 3.6 %collective-permute-start.5 = (bf16[128,128]{1,0:T(8,128)(2,1)S(1)}, bf16[128,128]{1,0:T(8,128)(2,1)S(1)}, u32[]{:S(2)}, u32[]{:S(2)}) collective-permute-start(bf16[128,128]{1,0:T(8,128)(2,1)S(1)} %get-tuple-element.15), channel_id=1, source_target_pairs={{4,0},{8,4},{12,8},{0,12},{5,1},{9,5},{13,9},{1,13},{6,2},{10,6},{... | collective-permute-start | bytes 98312 | tf_op jit(solution)/shard_map/ppermute | solution.py:433
  18.5 0.0 collective-permute-done.2.refs_3_
  18.5 0.0 collective-permute-done.3.refs_4_
  18.5 0.0 collective-permute-done.1.refs_2_
  18.5 2.2 %legendre_rows.1 = bf16[2,8,72,128]{3,2,1,0:T(8,128)(2,1)} custom-call(s32[5]{0:T(128)S(1)} %stack.23.place_ref, bf16[4,2,32,512]{3,2,1,0:T(8,128)(2,1)S(1)} %collective-permute-done.refs_0_, bf16[4,128,512]{2,1,0:T(8,128)(2,1)S(1)} %get-tuple-element.11.refs_1_, bf16[4,128,512]{2,1,0:T(8,128)(2,1)S(1)} %collective-permute-done.1.refs_2_, ...), custom_call_target="tpu_custom_call" | custom-call | tf_op jit(solution)/shard_map/legendre_rows/pallas_call | solution.py:187
  20.6 6.0 %all-to-all-start = ((bf16[16,72,128]{2,1,0:T(8,128)(2,1)}), bf16[16,72,128]{2,1,0:T(8,128)(2,1)S(1)}, u32[]{:S(2)}, u32[]{:S(2)}) async-start(bf16[16,72,128]{2,1,0:T(8,128)(2,1)} %bitcast.6), calls=%async_computation | async-start | bytes 589824 | tf_op jit(solution)/shard_map/all_to_all | solution.py:435
  26.6 3.5 %fusion.1.fourier_ref = bf16[12,128,128]{2,1,0:T(8,128)(2,1)S(1)} fusion(s32[12]{0:T(128)S(1)} %iota_multiply_fusion, s32[128]{0:T(128)S(1)} %get-tuple-element.19, s32[128]{0:T(128)S(1)} %get-tuple-element.22, s32[128]{0:T(128)S(1)} %get-tuple-element.20, s32[128]{0:T(128)S(1)} %get-tuple-element.23, s32[128]{0:T(128)S(1)} %get-tuple-element.21, ...), kind=kLoop, calls=%fused_computation.23 | loop fusion | flops 15335424 | bytes 396720 | tf_op jit(solution)/shard_map/convert_element_type | solution.py:400
  30.2 0.0 collective-permute-done.4.before_ref
  30.2 0.0 collective-permute-done.5.after_ref
  30.2 0.0 copy-done.3
  30.2 1.5 %block_weights.1.weights_ref = bf16[34,128,128]{2,1,0:T(8,128)(2,1)S(1)} custom-call(s32[5]{0:T(128)S(1)} %stack.23.place_ref, s32[4,32]{1,0:T(4,128)S(1)} %copy-done.3, bf16[12,128,128]{2,1,0:T(8,128)(2,1)S(1)} %fusion.1.fourier_ref, bf16[32,128,128]{2,1,0:T(8,128)(2,1)S(1)} %bitcast.14, bf16[128,128]{1,0:T(8,128)(2,1)S(1)} %collective-permute-done.4.before_ref, ...), custom_call_target="tpu_custom_call" | custom-call | tf_op jit(solution)/shard_map/block_weights/pallas_call | solution.py:282
  31.7 5.5 %all-to-all-done.spectral_ref = bf16[16,72,128]{2,1,0:T(8,128)(2,1)S(1)} async-done(((bf16[16,72,128]{2,1,0:T(8,128)(2,1)}), bf16[16,72,128]{2,1,0:T(8,128)(2,1)S(1)}, u32[]{:S(2)}, u32[]{:S(2)}) %all-to-all-start) | async-done | bytes 294944 | tf_op jit(solution)/shard_map/all_to_all | solution.py:435
  37.2 0.0 copy-done.1
  37.2 0.0 copy-done.2
  37.2 7.5 %patch_winds.1 = bf16[16,12288]{1,0:T(8,128)(2,1)} custom-call(bf16[16,72,128]{2,1,0:T(8,128)(2,1)S(1)} %all-to-all-done.spectral_ref, bf16[34,128,128]{2,1,0:T(8,128)(2,1)S(1)} %block_weights.1.weights_ref, s32[4,12288]{1,0:T(4,128)S(1)} %bitcast.15, f32[2,12288]{1,0:T(2,128)S(1)} %bitcast.16), custom_call_target="tpu_custom_call" | custom-call | tf_op jit(solution)/shard_map/patch_winds/pallas_call | solution.py:368
  (11 shorter events, 0.0 us)
Async XLA Ops:
  0.0 7.9 %copy-start = (bf16[1,32,128,128]{3,2,1,0:T(8,128)(2,1)S(1)}, bf16[1,32,128,128]{3,2,1,0:T(8,128)(2,1)}, u32[]{:S(2)}) copy-start(bf16[1,32,128,128]{3,2,1,0:T(8,128)(2,1)} %param.11) | copy-start | bytes 3145732
  0.0 30.2 %copy-start.3 = (s32[4,32]{1,0:T(4,128)S(1)}, s32[4,32]{1,0:T(4,128)}, u32[]{:S(2)}) copy-start(s32[4,32]{1,0:T(4,128)} %seg_ref.1) | copy-start | bytes 1540
  0.1 37.1 %copy-start.1 = (s32[1,4,12288]{2,1,0:T(4,128)S(1)}, s32[1,4,12288]{2,1,0:T(4,128)}, u32[]{:S(2)}) copy-start(s32[1,4,12288]{2,1,0:T(4,128)} %param.12) | copy-start | bytes 589828
  0.1 37.1 %copy-start.2 = (f32[1,2,12288]{2,1,0:T(2,128)S(1)}, f32[1,2,12288]{2,1,0:T(2,128)}, u32[]{:S(2)}) copy-start(f32[1,2,12288]{2,1,0:T(2,128)} %param.13) | copy-start | bytes 294916
  2.7 15.8 %collective-permute-start.1 = (bf16[4,128,512]{2,1,0:T(8,128)(2,1)S(1)}, bf16[4,128,512]{2,1,0:T(8,128)(2,1)S(1)}, u32[]{:S(2)}, u32[]{:S(2)}) collective-permute-start(bf16[4,128,512]{2,1,0:T(8,128)(2,1)S(1)} %get-tuple-element.11.refs_1_), channel_id=1, source_target_pairs={{0,2},{2,0},{1,3},{3,1},{4,6},{6,4},{5,7},{7,5},{8,10},{10,8},{9,1... | collective-permute-start | bytes 1572872 | tf_op jit(solution)/shard_map/ppermute | solution.py:427
  5.7 9.2 %collective-permute-start = (bf16[4,2,32,512]{3,2,1,0:T(8,128)(2,1)S(1)}, bf16[4,2,32,512]{3,2,1,0:T(8,128)(2,1)S(1)}, u32[]{:S(2)}, u32[]{:S(2)}) collective-permute-start(bf16[4,2,32,512]{3,2,1,0:T(8,128)(2,1)S(1)} %get-tuple-element.10), channel_id=1, source_target_pairs={{0,16},{1,17},{16,0},{17,1},{2,18},{3,19},{18,2},{19,3},{4,20},{5,... | collective-permute-start | bytes 786440 | tf_op jit(solution)/shard_map/ppermute | solution.py:423
  7.2 11.2 %collective-permute-start.2 = (bf16[4,2,32,512]{3,2,1,0:T(8,128)(2,1)S(1)}, bf16[4,2,32,512]{3,2,1,0:T(8,128)(2,1)S(1)}, u32[]{:S(2)}, u32[]{:S(2)}) collective-permute-start(bf16[4,2,32,512]{3,2,1,0:T(8,128)(2,1)S(1)} %get-tuple-element.12), channel_id=1, source_target_pairs={{0,17},{1,16},{16,1},{17,0},{2,19},{3,18},{18,3},{19,2},{4,21},{5,... | collective-permute-start | bytes 786440 | tf_op jit(solution)/shard_map/ppermute | solution.py:423
  7.2 11.2 %collective-permute-start.3 = (bf16[4,2,32,512]{3,2,1,0:T(8,128)(2,1)S(1)}, bf16[4,2,32,512]{3,2,1,0:T(8,128)(2,1)S(1)}, u32[]{:S(2)}, u32[]{:S(2)}) collective-permute-start(bf16[4,2,32,512]{3,2,1,0:T(8,128)(2,1)S(1)} %get-tuple-element.13), channel_id=1, source_target_pairs={{0,1},{1,0},{16,17},{17,16},{2,3},{3,2},{18,19},{19,18},{4,5},{5,4... | collective-permute-start | bytes 786440 | tf_op jit(solution)/shard_map/ppermute | solution.py:423
  7.9 22.3 %collective-permute-start.4 = (bf16[128,128]{1,0:T(8,128)(2,1)S(1)}, bf16[128,128]{1,0:T(8,128)(2,1)S(1)}, u32[]{:S(2)}, u32[]{:S(2)}) collective-permute-start(bf16[128,128]{1,0:T(8,128)(2,1)S(1)} %get-tuple-element.16), channel_id=1, source_target_pairs={{0,4},{4,8},{8,12},{12,0},{1,5},{5,9},{9,13},{13,1},{2,6},{6,10},{... | collective-permute-start | bytes 98312 | tf_op jit(solution)/shard_map/ppermute | solution.py:432
  14.9 15.3 %collective-permute-start.5 = (bf16[128,128]{1,0:T(8,128)(2,1)S(1)}, bf16[128,128]{1,0:T(8,128)(2,1)S(1)}, u32[]{:S(2)}, u32[]{:S(2)}) collective-permute-start(bf16[128,128]{1,0:T(8,128)(2,1)S(1)} %get-tuple-element.15), channel_id=1, source_target_pairs={{4,0},{8,4},{12,8},{0,12},{5,1},{9,5},{13,9},{1,13},{6,2},{10,6},{... | collective-permute-start | bytes 98312 | tf_op jit(solution)/shard_map/ppermute | solution.py:433
  20.6 16.5 %all-to-all-start = ((bf16[16,72,128]{2,1,0:T(8,128)(2,1)}), bf16[16,72,128]{2,1,0:T(8,128)(2,1)S(1)}, u32[]{:S(2)}, u32[]{:S(2)}) async-start(bf16[16,72,128]{2,1,0:T(8,128)(2,1)} %bitcast.6), calls=%async_computation | async-start | bytes 589824 | tf_op jit(solution)/shard_map/all_to_all | solution.py:435

commit v6 on v5

--- a/solution.py
+++ b/solution.py
@@ -40,11 +40,12 @@
     return pltpu.VMEM(shape, dtype) if fits(shape, dtype) else jax.ShapeDtypeStruct(shape, dtype)
 
 
-def select_kernel(place_ref, map_ref, legendre_ref, spectra_ref, out_ref, *refs, parts, pots):
+def select_kernel(map_ref, legendre_ref, spectra_ref, out_ref, *refs, parts, pots):
     *piece_refs, rows_ref, held_ref, sems = refs
     patches, blocks = rows_ref.shape
     wave_count, rows_dev, _ = held_ref.shape
-    share, lev, part, pot = place_ref[0], place_ref[1], place_ref[3], place_ref[4]
+    lev, part, pot = lax.axis_index("lev"), lax.axis_index("ens"), lax.axis_index("pot")
+    share = part * pots + pot
     rows_copy = pltpu.make_async_copy(map_ref, rows_ref, sems.at[wave_count])
     rows_copy.start()
     copies = [
@@ -87,7 +88,7 @@
         piece.wait()
 
 
-def select_rows(place, row_map, legendre, spectra, parts, pots):
+def select_rows(row_map, legendre, spectra, parts, pots):
     _, rows_dev, degrees = legendre.shape
     patches, blocks = row_map.shape
     waves, *rest = spectra.shape
@@ -97,7 +98,7 @@
         functools.partial(select_kernel, parts=parts, pots=pots),
         out_shape=[result((wave_count, patches * blocks, degrees), jnp.bfloat16)]
         + [result((wave_count, *rest), jnp.bfloat16)] * shares,
-        in_specs=[SCALARS, IN_HBM, IN_HBM, IN_HBM],
+        in_specs=[IN_HBM, IN_HBM, IN_HBM],
         out_specs=[WHOLE] * (1 + shares),
         scratch_shapes=[
             pltpu.VMEM((patches, blocks), jnp.int32),
@@ -106,13 +107,10 @@
         ],
         compiler_params=PARAMS,
         name="select_rows",
-    )(
-        place,
-        *(pltpu.with_memory_space_constraint(x, pltpu.HBM) for x in (row_map, legendre, spectra)),
-    )
-
-
-def legendre_kernel(place_ref, *refs, order, parts, pots, patches):
+    )(*(pltpu.with_memory_space_constraint(x, pltpu.HBM) for x in (row_map, legendre, spectra)))
+
+
+def legendre_kernel(*refs, order, parts, pots, patches):
     *given, out_ref, held_ref = refs
     shares = parts * pots
     spectra_refs = [given[order.index(k)] for k in range(shares)]
@@ -124,7 +122,7 @@
     groups = entries // (patches * SUB)
     lanes = groups * width
     rows = wave_count * pair
-    part = place_ref[3]
+    part = lax.axis_index("ens")
     rim = {}
     lane = lax.broadcasted_iota(jnp.int32, (1, lanes), 1)
     sub = lax.broadcasted_iota(jnp.int32, (rows, lanes), 0)
@@ -174,7 +172,7 @@
         out_ref[lax.rem(part + parts - e, parts)] = held_ref[e]
 
 
-def legendre_rows(place, tables, spectra, parts, pots, patches):
+def legendre_rows(tables, spectra, parts, pots, patches):
     shares = parts * pots
     across = range(pots, shares, pots)
     order = [*across, *range(shares, shares + len(tables))]
@@ -189,14 +187,14 @@
             legendre_kernel, order=order, parts=parts, pots=pots, patches=patches
         ),
         out_shape=result((parts, patches * pots, rows * SUB + rows, lanes), jnp.bfloat16),
-        in_specs=[SCALARS] + [WHOLE] * len(given),
+        in_specs=[WHOLE] * len(given),
         out_specs=WHOLE,
         scratch_shapes=[
             pltpu.VMEM((parts, patches * pots, rows * SUB + rows, lanes), jnp.bfloat16)
         ],
         compiler_params=PARAMS,
         name="legendre_rows",
-    )(place, *in_vmem(*given)).reshape(parts * patches * pots, rows * SUB + rows, lanes)
+    )(*in_vmem(*given)).reshape(parts * patches * pots, rows * SUB + rows, lanes)
 
 
 def lane_gather(values, index):
@@ -262,9 +260,9 @@
     return [at[1] - at[0], at[3] - at[2]]
 
 
-def weights_kernel(place_ref, seg_ref, fourier_ref, interp_ref, before_ref, after_ref, out_ref):
+def weights_kernel(seg_ref, fourier_ref, interp_ref, before_ref, after_ref, out_ref):
     patches, blocks = seg_ref.shape
-    own = place_ref[2]
+    own = lax.axis_index("wave")
 
     def block_weights(segment, weights):
         return dot_nt(fourier_ref[segment], weights).astype(jnp.bfloat16)
@@ -277,16 +275,16 @@
     out_ref[blocks + 1] = block_weights(seg_ref[after, 0], after_ref[...])
 
 
-def block_weights(place, seg_map, fourier, interp, before, after):
+def block_weights(seg_map, fourier, interp, before, after):
     blocks = interp.shape[0]
     return pl.pallas_call(
         weights_kernel,
         out_shape=result((blocks + 2, fourier.shape[1], BLOCK), jnp.bfloat16),
-        in_specs=[SCALARS, SCALARS] + [WHOLE] * 4,
+        in_specs=[SCALARS] + [WHOLE] * 4,
         out_specs=WHOLE,
         compiler_params=PARAMS,
         name="block_weights",
-    )(place, seg_map, *in_vmem(fourier, interp, before, after))
+    )(seg_map, *in_vmem(fourier, interp, before, after))
 
 
 def patch_kernel(
@@ -407,13 +405,7 @@
     own_waves, pair, level_count, degrees = own_spectra.shape
     shares = parts * pots
     wave_count = own_waves // shares
-    share = lax.axis_index("ens") * pots + lax.axis_index("pot")
-    own = lax.axis_index("wave")
-
-    part, pot = lax.axis_index("ens"), lax.axis_index("pot")
-    place = jnp.stack([share, lax.axis_index("lev"), own, part, pot]).astype(jnp.int32)
-
-    chosen, *pieces = select_rows(place, row_map, legendre, own_spectra, parts, pots)
+    chosen, *pieces = select_rows(row_map, legendre, own_spectra, parts, pots)
     def deal(k):
         pairs = [
             (i * pots + j, (i + k // pots) % parts * pots + (j + k % pots) % pots)
@@ -431,12 +423,12 @@
     gathered = [pieces[0]] + [dealt[k] for k in range(1, shares)]
     before = lax.ppermute(interp[0, -1], "wave", [(i, (i + 1) % waves) for i in range(waves)])
     after = lax.ppermute(interp[0, 0], "wave", [((i + 1) % waves, i) for i in range(waves)])
-    outgoing = legendre_rows(place, tables, gathered, parts, pots, row_map.shape[0])
+    outgoing = legendre_rows(tables, gathered, parts, pots, row_map.shape[0])
     incoming = lax.all_to_all(
         outgoing, ("ens", "wave", "pot"), split_axis=0, concat_axis=0, tiled=True
     )
     fourier = fourier_segments(parts, waves, pots, wave_count, own_waves)
-    weights = block_weights(place, seg_map, fourier, interp[0], before, after)
+    weights = block_weights(seg_map, fourier, interp[0], before, after)
     return patch_winds(incoming, weights, edges[0], inv_len[0], pots)
 
 

time: 44.9 us -> 43.8 us (0.976)
  Pallas kernels: 13.7 us -> 12.7 us
    pallas_call x1, Pallas kernels: 2.16 us -> 1.62 us  [legendre_rows(): pl.pallas_call(functools.partial(legendre_kernel, order=order, parts=part...]
  transfers between devices with their start and end apart: 7 -> 7, of which waited for: 2 -> 2; matrix products, arithmetic and copies ran while one was open for 8% -> 8% of each run, Pallas kernels for 8% -> 7%
where the time goes in v6:
time: 43.8 us; the launch traced here: 43.6 us
  starting transfers between devices  16.4 us (37%)
  Pallas kernels  12.7 us (29%)
  waiting for transfers between devices  10.9 us (25%)
  other arithmetic  3.56 us (8%)
    pallas_call x1, Pallas kernels, patch_winds(): pl.pallas_call(patch_kernel, out_shape=jax.ShapeDtypeStruct((half, edges....  7.51 us
    all_to_all x1, starting transfers between devices, body(): lax.all_to_all(outgoing, ('ens', 'wave', 'pot'), split_axis=0, concat_axi...  5.97 us
    all_to_all x1, waiting for transfers between devices, body(): lax.all_to_all(outgoing, ('ens', 'wave', 'pot'), split_axis=0, concat_axi...  5.5 us
    ppermute x3, waiting for transfers between devices, deal(): return lax.ppermute(pieces[k], ('ens', 'pot'), pairs)  5.34 us
    ppermute x1, starting transfers between devices, body(): lax.ppermute(interp[0, 0], 'wave', [((i + 1) % waves, i) for i in range(w...  3.6 us
    convert_element_type x1, other arithmetic, fourier_segments(): return jnp.where(mode % 2 == 0, factor * jnp.cos(angle_values), -factor *...  3.53 us
    ppermute x1, starting transfers between devices, body(): lax.ppermute(chosen, 'lev', [(i, (i + step) % levs) for i in range(levs)])  3.04 us
    ppermute x3, starting transfers between devices, deal(): return lax.ppermute(pieces[k], ('ens', 'pot'), pairs)  2.14 us
  transfers between devices with their start and end apart: 7, of which 2 were waited for; matrix products, arithmetic and copies ran while one was open for 8% of the time, Pallas kernels for 7%

profile of v6, /device:TPU:0, one launch (start us, length us, event | category | flops | bytes accessed | tf_op | source)
XLA Modules:
  0.0 43.6 jit_solution(16791867477643586133)
XLA Ops:
  0.0 0.0 copy-start
  0.0 2.1 %select_rows.1 = (bf16[4,128,512]{2,1,0:T(8,128)(2,1)S(1)}, bf16[4,2,32,512]{3,2,1,0:T(8,128)(2,1)S(1)}, bf16[4,2,32,512]{3,2,1,0:T(8,128)(2,1)S(1)}, bf16[4,2,3...) custom-call(s32[4,32]{1,0:T(4,128)} %map_ref.1, bf16[16,384,512]{2,1,0:T(8,128)(2,1)} %legendre_ref.1, ...), custom_call_target="tpu_custom_call" | custom-call | tf_op jit(solution)/shard_map/select_rows/pallas_call | solution.py:97
  2.1 3.0 %collective-permute-start.1 = (bf16[4,128,512]{2,1,0:T(8,128)(2,1)S(1)}, bf16[4,128,512]{2,1,0:T(8,128)(2,1)S(1)}, u32[]{:S(2)}, u32[]{:S(2)}) collective-permute-start(bf16[4,128,512]{2,1,0:T(8,128)(2,1)S(1)} %get-tuple-element.11.refs_1_), channel_id=1, source_target_pairs={{0,2},{2,0},{1,3},{3,1},{4,6},{6,4},{5,7},{7,5},{8,10},{10,8},{9,1... | collective-permute-start | bytes 1572872 | tf_op jit(solution)/shard_map/ppermute | solution.py:419
  5.2 1.5 %collective-permute-start = (bf16[4,2,32,512]{3,2,1,0:T(8,128)(2,1)S(1)}, bf16[4,2,32,512]{3,2,1,0:T(8,128)(2,1)S(1)}, u32[]{:S(2)}, u32[]{:S(2)}) collective-permute-start(bf16[4,2,32,512]{3,2,1,0:T(8,128)(2,1)S(1)} %get-tuple-element.10), channel_id=1, source_target_pairs={{0,16},{1,17},{16,0},{17,1},{2,18},{3,19},{18,2},{19,3},{4,20},{5,... | collective-permute-start | bytes 786440 | tf_op jit(solution)/shard_map/ppermute | solution.py:415
  6.7 0.0 collective-permute-start.2
  6.7 0.6 %collective-permute-start.3 = (bf16[4,2,32,512]{3,2,1,0:T(8,128)(2,1)S(1)}, bf16[4,2,32,512]{3,2,1,0:T(8,128)(2,1)S(1)}, u32[]{:S(2)}, u32[]{:S(2)}) collective-permute-start(bf16[4,2,32,512]{3,2,1,0:T(8,128)(2,1)S(1)} %get-tuple-element.13), channel_id=1, source_target_pairs={{0,1},{1,0},{16,17},{17,16},{2,3},{3,2},{18,19},{19,18},{4,5},{5,4... | collective-permute-start | bytes 786440 | tf_op jit(solution)/shard_map/ppermute | solution.py:415
  7.3 0.0 copy-done
  7.3 1.6 %collective-permute-start.4 = (bf16[128,128]{1,0:T(8,128)(2,1)S(1)}, bf16[128,128]{1,0:T(8,128)(2,1)S(1)}, u32[]{:S(2)}, u32[]{:S(2)}) collective-permute-start(bf16[128,128]{1,0:T(8,128)(2,1)S(1)} %get-tuple-element.16), channel_id=1, source_target_pairs={{0,4},{4,8},{8,12},{12,0},{1,5},{5,9},{9,13},{13,1},{2,6},{6,10},{... | collective-permute-start | bytes 98312 | tf_op jit(solution)/shard_map/ppermute | solution.py:424
  9.0 5.3 %collective-permute-done.refs_0_ = bf16[4,2,32,512]{3,2,1,0:T(8,128)(2,1)S(1)} collective-permute-done((bf16[4,2,32,512]{3,2,1,0:T(8,128)(2,1)S(1)}, bf16[4,2,32,512]{3,2,1,0:T(8,128)(2,1)S(1)}, u32[]{:S(2)}, u32[]{:S(2)}) %collective-permute-start) | collective-permute-done | bytes 262176 | tf_op jit(solution)/shard_map/ppermute | solution.py:415
  14.4 3.6 %collective-permute-start.5 = (bf16[128,128]{1,0:T(8,128)(2,1)S(1)}, bf16[128,128]{1,0:T(8,128)(2,1)S(1)}, u32[]{:S(2)}, u32[]{:S(2)}) collective-permute-start(bf16[128,128]{1,0:T(8,128)(2,1)S(1)} %get-tuple-element.15), channel_id=1, source_target_pairs={{4,0},{8,4},{12,8},{0,12},{5,1},{9,5},{13,9},{1,13},{6,2},{10,6},{... | collective-permute-start | bytes 98312 | tf_op jit(solution)/shard_map/ppermute | solution.py:425
  18.0 0.0 collective-permute-done.2.refs_3_
  18.0 0.0 collective-permute-done.3.refs_4_
  18.0 0.0 collective-permute-done.1.refs_2_
  18.0 1.6 %legendre_rows.1 = bf16[2,8,72,128]{3,2,1,0:T(8,128)(2,1)} custom-call(bf16[4,2,32,512]{3,2,1,0:T(8,128)(2,1)S(1)} %collective-permute-done.refs_0_, bf16[4,128,512]{2,1,0:T(8,128)(2,1)S(1)} %get-tuple-element.11.refs_1_, bf16[4,128,512]{2,1,0:T(8,128)(2,1)S(1)} %collective-permute-done.1.refs_2_, ...), custom_call_target="tpu_custom_call" | custom-call | tf_op jit(solution)/shard_map/legendre_rows/pallas_call | solution.py:185
  19.6 6.0 %all-to-all-start = ((bf16[16,72,128]{2,1,0:T(8,128)(2,1)}), bf16[16,72,128]{2,1,0:T(8,128)(2,1)S(1)}, u32[]{:S(2)}, u32[]{:S(2)}) async-start(bf16[16,72,128]{2,1,0:T(8,128)(2,1)} %bitcast.1), calls=%async_computation | async-start | bytes 589824 | tf_op jit(solution)/shard_map/all_to_all | solution.py:427
  25.6 3.5 %fusion.1.fourier_ref = bf16[12,128,128]{2,1,0:T(8,128)(2,1)S(1)} fusion(s32[12]{0:T(128)S(1)} %iota_multiply_fusion, s32[128]{0:T(128)S(1)} %get-tuple-element.19, s32[128]{0:T(128)S(1)} %get-tuple-element.22, s32[128]{0:T(128)S(1)} %get-tuple-element.20, s32[128]{0:T(128)S(1)} %get-tuple-element.23, s32[128]{0:T(128)S(1)} %get-tuple-element.21, ...), kind=kLoop, calls=%fused_computation.23 | loop fusion | flops 15335424 | bytes 396720 | tf_op jit(solution)/shard_map/convert_element_type | solution.py:398
  29.1 0.0 collective-permute-done.4.before_ref
  29.1 0.0 collective-permute-done.5.after_ref
  29.1 0.0 copy-done.3
  29.1 1.5 %block_weights.1.weights_ref = bf16[34,128,128]{2,1,0:T(8,128)(2,1)S(1)} custom-call(s32[4,32]{1,0:T(4,128)S(1)} %copy-done.3, bf16[12,128,128]{2,1,0:T(8,128)(2,1)S(1)} %fusion.1.fourier_ref, bf16[32,128,128]{2,1,0:T(8,128)(2,1)S(1)} %bitcast.9, bf16[128,128]{1,0:T(8,128)(2,1)S(1)} %collective-permute-done.4.before_ref, ...), custom_call_target="tpu_custom_call" | custom-call | tf_op jit(solution)/shard_map/block_weights/pallas_call | solution.py:280
  30.6 5.5 %all-to-all-done.spectral_ref = bf16[16,72,128]{2,1,0:T(8,128)(2,1)S(1)} async-done(((bf16[16,72,128]{2,1,0:T(8,128)(2,1)}), bf16[16,72,128]{2,1,0:T(8,128)(2,1)S(1)}, u32[]{:S(2)}, u32[]{:S(2)}) %all-to-all-start) | async-done | bytes 294944 | tf_op jit(solution)/shard_map/all_to_all | solution.py:427
  36.1 0.0 copy-done.1
  36.1 0.0 copy-done.2
  36.1 7.5 %patch_winds.1 = bf16[16,12288]{1,0:T(8,128)(2,1)} custom-call(bf16[16,72,128]{2,1,0:T(8,128)(2,1)S(1)} %all-to-all-done.spectral_ref, bf16[34,128,128]{2,1,0:T(8,128)(2,1)S(1)} %block_weights.1.weights_ref, s32[4,12288]{1,0:T(4,128)S(1)} %bitcast.10, f32[2,12288]{1,0:T(2,128)S(1)} %bitcast.11), custom_call_target="tpu_custom_call" | custom-call | tf_op jit(solution)/shard_map/patch_winds/pallas_call | solution.py:366
  (10 shorter events, 0.0 us)
Async XLA Ops:
  0.0 7.3 %copy-start = (bf16[1,32,128,128]{3,2,1,0:T(8,128)(2,1)S(1)}, bf16[1,32,128,128]{3,2,1,0:T(8,128)(2,1)}, u32[]{:S(2)}) copy-start(bf16[1,32,128,128]{3,2,1,0:T(8,128)(2,1)} %param.11) | copy-start | bytes 3145732
  0.0 29.1 %copy-start.3 = (s32[4,32]{1,0:T(4,128)S(1)}, s32[4,32]{1,0:T(4,128)}, u32[]{:S(2)}) copy-start(s32[4,32]{1,0:T(4,128)} %seg_ref.1) | copy-start | bytes 1540
  0.0 36.1 %copy-start.1 = (s32[1,4,12288]{2,1,0:T(4,128)S(1)}, s32[1,4,12288]{2,1,0:T(4,128)}, u32[]{:S(2)}) copy-start(s32[1,4,12288]{2,1,0:T(4,128)} %param.12) | copy-start | bytes 589828
  0.0 36.1 %copy-start.2 = (f32[1,2,12288]{2,1,0:T(2,128)S(1)}, f32[1,2,12288]{2,1,0:T(2,128)}, u32[]{:S(2)}) copy-start(f32[1,2,12288]{2,1,0:T(2,128)} %param.13) | copy-start | bytes 294916
  2.1 15.8 %collective-permute-start.1 = (bf16[4,128,512]{2,1,0:T(8,128)(2,1)S(1)}, bf16[4,128,512]{2,1,0:T(8,128)(2,1)S(1)}, u32[]{:S(2)}, u32[]{:S(2)}) collective-permute-start(bf16[4,128,512]{2,1,0:T(8,128)(2,1)S(1)} %get-tuple-element.11.refs_1_), channel_id=1, source_target_pairs={{0,2},{2,0},{1,3},{3,1},{4,6},{6,4},{5,7},{7,5},{8,10},{10,8},{9,1... | collective-permute-start | bytes 1572872 | tf_op jit(solution)/shard_map/ppermute | solution.py:419
  5.2 9.2 %collective-permute-start = (bf16[4,2,32,512]{3,2,1,0:T(8,128)(2,1)S(1)}, bf16[4,2,32,512]{3,2,1,0:T(8,128)(2,1)S(1)}, u32[]{:S(2)}, u32[]{:S(2)}) collective-permute-start(bf16[4,2,32,512]{3,2,1,0:T(8,128)(2,1)S(1)} %get-tuple-element.10), channel_id=1, source_target_pairs={{0,16},{1,17},{16,0},{17,1},{2,18},{3,19},{18,2},{19,3},{4,20},{5,... | collective-permute-start | bytes 786440 | tf_op jit(solution)/shard_map/ppermute | solution.py:415
  6.7 11.3 %collective-permute-start.2 = (bf16[4,2,32,512]{3,2,1,0:T(8,128)(2,1)S(1)}, bf16[4,2,32,512]{3,2,1,0:T(8,128)(2,1)S(1)}, u32[]{:S(2)}, u32[]{:S(2)}) collective-permute-start(bf16[4,2,32,512]{3,2,1,0:T(8,128)(2,1)S(1)} %get-tuple-element.12), channel_id=1, source_target_pairs={{0,17},{1,16},{16,1},{17,0},{2,19},{3,18},{18,3},{19,2},{4,21},{5,... | collective-permute-start | bytes 786440 | tf_op jit(solution)/shard_map/ppermute | solution.py:415
  6.7 11.3 %collective-permute-start.3 = (bf16[4,2,32,512]{3,2,1,0:T(8,128)(2,1)S(1)}, bf16[4,2,32,512]{3,2,1,0:T(8,128)(2,1)S(1)}, u32[]{:S(2)}, u32[]{:S(2)}) collective-permute-start(bf16[4,2,32,512]{3,2,1,0:T(8,128)(2,1)S(1)} %get-tuple-element.13), channel_id=1, source_target_pairs={{0,1},{1,0},{16,17},{17,16},{2,3},{3,2},{18,19},{19,18},{4,5},{5,4... | collective-permute-start | bytes 786440 | tf_op jit(solution)/shard_map/ppermute | solution.py:415
  7.3 21.8 %collective-permute-start.4 = (bf16[128,128]{1,0:T(8,128)(2,1)S(1)}, bf16[128,128]{1,0:T(8,128)(2,1)S(1)}, u32[]{:S(2)}, u32[]{:S(2)}) collective-permute-start(bf16[128,128]{1,0:T(8,128)(2,1)S(1)} %get-tuple-element.16), channel_id=1, source_target_pairs={{0,4},{4,8},{8,12},{12,0},{1,5},{5,9},{9,13},{13,1},{2,6},{6,10},{... | collective-permute-start | bytes 98312 | tf_op jit(solution)/shard_map/ppermute | solution.py:424
  14.4 14.8 %collective-permute-start.5 = (bf16[128,128]{1,0:T(8,128)(2,1)S(1)}, bf16[128,128]{1,0:T(8,128)(2,1)S(1)}, u32[]{:S(2)}, u32[]{:S(2)}) collective-permute-start(bf16[128,128]{1,0:T(8,128)(2,1)S(1)} %get-tuple-element.15), channel_id=1, source_target_pairs={{4,0},{8,4},{12,8},{0,12},{5,1},{9,5},{13,9},{1,13},{6,2},{10,6},{... | collective-permute-start | bytes 98312 | tf_op jit(solution)/shard_map/ppermute | solution.py:425
  19.6 16.5 %all-to-all-start = ((bf16[16,72,128]{2,1,0:T(8,128)(2,1)}), bf16[16,72,128]{2,1,0:T(8,128)(2,1)S(1)}, u32[]{:S(2)}, u32[]{:S(2)}) async-start(bf16[16,72,128]{2,1,0:T(8,128)(2,1)} %bitcast.1), calls=%async_computation | async-start | bytes 589824 | tf_op jit(solution)/shard_map/all_to_all | solution.py:427
